TPU v7x, 32 devices: a whole 2x2x4 slice. The times are simulated.
32 devices in a mesh: dp: 4 (over z), row: 4 (over x, core), col: 2 (over y).
Axes of the slice: x: 2, y: 2, z: 4, core: 2. Of those that a mesh axis runs over, the one named last changes fastest.
Arguments:
- tokens: bfloat16 [4096, 1024], P(('dp', 'col'), 'row'), may hold values from -6 to 6
- cotangent: bfloat16 [4096, 1024], P(('dp', 'col'), 'row'), may hold values from -6 to 6
- seg_ids: int32 [4, 1024], P('dp'), may hold values from 0 to 6, never falling along the last dimension, each value on 1 to 256 neighbouring positions
- norm_one: float32 [1024], P('row'), may hold values from 0.1 to 1.9
- wq: bfloat16 [1024, 1024], P('row', 'col'), may hold values from -0.1875 to 0.1875
- wk: bfloat16 [1024, 1024], P('row', 'col'), may hold values from -0.1875 to 0.1875
- wv: bfloat16 [1024, 1024], P('row', 'col'), may hold values from -0.1875 to 0.1875
- wo: bfloat16 [1024, 1024], P('col', 'row'), may hold values from -2 to 2
- norm_two: float32 [1024], P('row'), may hold values from 0.1 to 1.9
- w_gate: bfloat16 [1024, 2816], P('row', 'col'), may hold values from -0.1875 to 0.1875
- w_up: bfloat16 [1024, 2816], P('row', 'col'), may hold values from -0.1875 to 0.1875
- w_down: bfloat16 [2816, 1024], P('col', 'row'), may hold values from -0.109375 to 0.109375
Outputs:
- output: bfloat16 [4096, 1024], P(('dp', 'col'), 'row')
- grad_input: float32 [4096, 1024], P(('dp', 'col'), 'row')
- grad_norm_one: float32 [1024], P('row')
- grad_wq: float32 [1024, 1024], P('row', 'col')
- grad_wk: float32 [1024, 1024], P('row', 'col')
- grad_wv: float32 [1024, 1024], P('row', 'col')
- grad_wo: float32 [1024, 1024], P('col', 'row')
- grad_norm_two: float32 [1024], P('row')
- grad_gate: float32 [1024, 2816], P('row', 'col')
- grad_up: float32 [1024, 2816], P('row', 'col')
- grad_down: float32 [2816, 1024], P('col', 'row')
Inputs may be any that keep to these rules, and one draw needn't show every extreme that they name: Along each row of seg_ids the ids start at 0 and never fall; each sequence covers 1 to 256 positions and one covers exactly 256.
All inputs are finite; a program needn't handle non-finite values.
Results may differ from a plain program's by a relative error of at most 0.04.
Values may be sent and summed in bfloat16 or wider, within the bound.
A program may use at most 128 MiB of HBM per device.

v0:
```python
import jax
import jax.numpy as jnp
from jax import lax
from jax.sharding import PartitionSpec as P

D = 1024
HEAD_DIM = 64


EPSILON = 1e-05
NEGATIVE = -1e30


def for_sending(array):

    def short(part):
        return part.astype(jnp.bfloat16) if part.dtype == jnp.float32 else part

    return jax.tree.map(short, array)


def shifted(block, axis, distance):
    devices = range(lax.axis_size(axis))
    route = [(i - distance, i) for i in devices if i - distance in devices]
    return lax.ppermute(block, axis, route)


def matmul(first_op, second_op):
    return jnp.dot(first_op, second_op, preferred_element_type=jnp.float32)


def matmul_tn(first_op, second_op):
    return lax.dot_general(
        first_op, second_op, (((0,), (0,)), ((), ())), preferred_element_type=jnp.float32
    )


def matmul_nt(first_op, second_op):
    return lax.dot_general(
        first_op, second_op, (((1,), (1,)), ((), ())), preferred_element_type=jnp.float32
    )


def tokens_col(array_in):
    return lax.all_gather(array_in, "col", axis=0, tiled=True)


def tokens_row(array_in):
    return lax.all_gather(for_sending(array_in), "row", axis=0, tiled=True).astype(array_in.dtype)


def summed_row(array_in):
    return lax.psum_scatter(
        array_in.astype(jnp.bfloat16), "row", scatter_dimension=0, tiled=True
    ).astype(jnp.float32)


def summed_col(array_in):
    return lax.psum_scatter(
        array_in.astype(jnp.bfloat16), "col", scatter_dimension=0, tiled=True
    ).astype(jnp.float32)


def feature_total(array_in):
    return lax.psum(array_in, "row")


def window_parts(queries, keys_all, ids_ext, offset, head_cols):
    t_local = queries.shape[0]
    block_rows = min(512, t_local)
    key_reach = min(2048, t_local)
    window = key_reach + block_rows
    head_count = head_cols // HEAD_DIM
    anchor = offset + t_local - key_reach
    q_blk = lax.dynamic_slice_in_dim(queries, offset, block_rows, 0).reshape(
        block_rows, head_count, HEAD_DIM
    )
    k_win = lax.dynamic_slice_in_dim(keys_all, anchor, window, 0)
    k_blk = k_win[:, :head_cols].reshape(window, head_count, HEAD_DIM)
    v_blk = k_win[:, head_cols:].reshape(window, head_count, HEAD_DIM)
    q_ids = lax.dynamic_slice_in_dim(ids_ext, offset + t_local, block_rows, 0)
    k_ids = lax.dynamic_slice_in_dim(ids_ext, anchor, window, 0)
    q_pos = offset + lax.iota(jnp.int32, block_rows)
    k_pos = offset - key_reach + lax.iota(jnp.int32, window)
    allowed = (q_ids[:, None] == k_ids[None, :]) & (k_pos[None, :] <= q_pos[:, None])
    scores = jnp.einsum(
        "qhd,khd->hqk", q_blk, k_blk, preferred_element_type=jnp.float32
    ) * HEAD_DIM ** (-0.5)
    scores = jnp.where(allowed[None], scores, NEGATIVE)
    return (q_blk, k_blk, v_blk, scores)


def forward(tokens, seg_ids, norm_one, wq, wk, wv, wo, norm_two, w_gate, w_up, w_down):
    token_vals = tokens.astype(jnp.float32)
    scale_one = lax.rsqrt(feature_total(jnp.sum(token_vals * token_vals, axis=1)) / D + EPSILON)
    normed = (token_vals * scale_one[:, None] * norm_one).astype(jnp.bfloat16)
    normed_all = tokens_col(normed)
    w_qkv = jnp.concatenate([wq, wk, wv], axis=1)
    head_cols = wq.shape[1]
    qkv = summed_row(matmul(normed_all, w_qkv)).astype(jnp.bfloat16)
    queries = qkv[:, :head_cols]
    kv_local = qkv[:, head_cols:]
    prior_keys = shifted(kv_local, "row", 1)
    keys_all = jnp.concatenate([prior_keys, kv_local], axis=0)
    t_local = queries.shape[0]
    block_rows = min(512, t_local)
    padded_ids = jnp.concatenate([jnp.full((t_local,), -1, jnp.int32), seg_ids[0]])
    ids_ext = lax.dynamic_slice_in_dim(padded_ids, lax.axis_index("row") * t_local, 2 * t_local, 0)

    def attend(offset):
        q_blk, k_blk, v_blk, scores = window_parts(queries, keys_all, ids_ext, offset, head_cols)
        row_max = jnp.max(scores, axis=2, keepdims=True)
        exp_total = jnp.sum(jnp.exp(scores - row_max), axis=2, keepdims=True)
        log_total = row_max + jnp.log(exp_total)
        prob_low = jnp.exp(scores - log_total).astype(jnp.bfloat16)
        mixed_out = jnp.einsum("hqk,khd->qhd", prob_low, v_blk, preferred_element_type=jnp.float32)
        return (mixed_out.reshape(block_rows, head_cols).astype(jnp.bfloat16), log_total[:, :, 0])

    offsets = lax.iota(jnp.int32, t_local // block_rows) * block_rows
    pieces, log_totals = lax.map(attend, offsets)
    attn_out = pieces.reshape(t_local, head_cols)
    attn_all = tokens_row(attn_out)
    residual = token_vals + summed_col(matmul(attn_all, wo))
    stored = {
        "token_vals": token_vals,
        "scale_one": scale_one,
        "normed_all": normed_all,
        "queries": queries,
        "keys_all": keys_all,
        "ids_ext": ids_ext,
        "log_totals": log_totals,
        "attn_all": attn_all,
        "offsets": offsets,
    }
    f_col = w_gate.shape[1]
    scale_two = lax.rsqrt(feature_total(jnp.sum(residual * residual, axis=1)) / D + EPSILON)
    hidden_in = (residual * scale_two[:, None] * norm_two).astype(jnp.bfloat16)
    hidden_all = tokens_col(hidden_in)
    w_pair = jnp.concatenate([w_gate, w_up], axis=1)
    pair_sum = summed_row(matmul(hidden_all, w_pair))
    gate_pre = pair_sum[:, :f_col]
    up_pre = pair_sum[:, f_col:]
    act_low = (jax.nn.silu(gate_pre) * up_pre).astype(jnp.bfloat16)
    act_all = tokens_row(act_low)
    final_sum = residual + summed_col(matmul(act_all, w_down))
    stored.update(
        {
            "residual": residual,
            "scale_two": scale_two,
            "hidden_all": hidden_all,
            "gate_pre": gate_pre,
            "up_pre": up_pre,
            "act_all": act_all,
        }
    )
    return (final_sum.astype(jnp.bfloat16), stored)


def swiglu_grads(dact, gate_pre, up_pre):
    sigmoid_gate = jax.nn.sigmoid(gate_pre)
    gate_grad = (dact * up_pre * sigmoid_gate * (1.0 + gate_pre * (1.0 - sigmoid_gate))).astype(
        jnp.bfloat16
    )
    up_grad = (dact * gate_pre * sigmoid_gate).astype(jnp.bfloat16)
    return (gate_grad, up_grad)


def per_device(
    tokens, cotangent, seg_ids, norm_one, wq, wk, wv, wo, norm_two, w_gate, w_up, w_down
):
    weights = (tokens, seg_ids, norm_one, wq, wk, wv, wo, norm_two, w_gate, w_up, w_down)
    output, stored = forward(*weights)
    f_col = w_gate.shape[1]
    grad_out = cotangent.astype(jnp.float32)
    grad_all = tokens_col(cotangent)
    dact = summed_row(matmul_nt(grad_all, w_down))
    grad_down = matmul_tn(stored["act_all"], grad_all)
    gate_grad, up_grad = swiglu_grads(dact, stored["gate_pre"], stored["up_pre"])
    dpair = jnp.concatenate([gate_grad, up_grad], axis=1)
    dpair_all = tokens_row(dpair)
    w_pair = jnp.concatenate([w_gate, w_up], axis=1)
    dhidden = summed_col(matmul_nt(dpair_all, w_pair))
    grad_pair = matmul_tn(stored["hidden_all"], dpair_all)
    grad_gate = grad_pair[:, :f_col]
    grad_up = grad_pair[:, f_col:]
    residual = stored["residual"]
    scale_two = stored["scale_two"]
    weighted = dhidden * norm_two
    inner_sum = feature_total(jnp.sum(weighted * residual, axis=1)) / D
    dresid = (
        grad_out + scale_two[:, None] * weighted - residual * (scale_two**3 * inner_sum)[:, None]
    )
    grad_norm_two = jnp.sum(dhidden * residual * scale_two[:, None], axis=0)
    dbranch = dresid.astype(jnp.bfloat16)
    dbranch_all = tokens_col(dbranch)
    attn_grad = summed_row(matmul_nt(dbranch_all, wo)).astype(jnp.bfloat16)
    grad_wo = matmul_tn(stored["attn_all"], dbranch_all)
    queries = stored["queries"]
    keys_all = stored["keys_all"]
    ids_ext = stored["ids_ext"]
    head_cols = wq.shape[1]
    head_count = head_cols // HEAD_DIM
    t_local = queries.shape[0]
    block_rows = min(512, t_local)
    key_reach = min(2048, t_local)
    window = key_reach + block_rows
    inv_root = HEAD_DIM ** (-0.5)

    def attend_back(accum_dkv, inputs):
        offset, log_total = inputs
        q_blk, k_blk, v_blk, scores = window_parts(queries, keys_all, ids_ext, offset, head_cols)
        prob_full = jnp.exp(scores - log_total[:, :, None])
        prob_low = prob_full.astype(jnp.bfloat16)
        d_blk = lax.dynamic_slice_in_dim(attn_grad, offset, block_rows, 0).reshape(
            block_rows, head_count, HEAD_DIM
        )
        dprobs = jnp.einsum("qhd,khd->hqk", d_blk, v_blk, preferred_element_type=jnp.float32)
        dvalue = jnp.einsum("hqk,qhd->khd", prob_low, d_blk, preferred_element_type=jnp.float32)
        center = jnp.sum(prob_full * dprobs, axis=2, keepdims=True)
        dscores = (prob_full * (dprobs - center)).astype(jnp.bfloat16)
        dquery = (
            jnp.einsum("hqk,khd->qhd", dscores, k_blk, preferred_element_type=jnp.float32)
            * inv_root
        )
        dkey = (
            jnp.einsum("hqk,qhd->khd", dscores, q_blk, preferred_element_type=jnp.float32)
            * inv_root
        )
        update = jnp.concatenate(
            [dkey.reshape(window, head_cols), dvalue.reshape(window, head_cols)], axis=1
        )
        anchor = offset + t_local - key_reach
        current = lax.dynamic_slice_in_dim(accum_dkv, anchor, window, 0)
        accum_dkv = lax.dynamic_update_slice_in_dim(accum_dkv, current + update, anchor, 0)
        return (accum_dkv, dquery.reshape(block_rows, head_cols))

    start_grads = jnp.zeros((2 * t_local, 2 * head_cols), jnp.float32)
    accum_dkv, query_grads = lax.scan(
        attend_back, start_grads, (stored["offsets"], stored["log_totals"])
    )
    returned = shifted(accum_dkv[:t_local].astype(jnp.bfloat16), "row", -1).astype(jnp.float32)
    key_grads = accum_dkv[t_local:] + returned
    dqkv = jnp.concatenate([query_grads.reshape(t_local, head_cols), key_grads], axis=1).astype(
        jnp.bfloat16
    )
    dqkv_all = tokens_row(dqkv)
    w_qkv = jnp.concatenate([wq, wk, wv], axis=1)
    dnormed = summed_col(matmul_nt(dqkv_all, w_qkv))
    grad_qkv = matmul_tn(stored["normed_all"], dqkv_all)
    grad_wq = grad_qkv[:, :head_cols]
    grad_wk = grad_qkv[:, head_cols : 2 * head_cols]
    grad_wv = grad_qkv[:, 2 * head_cols :]
    token_vals = stored["token_vals"]
    scale_one = stored["scale_one"]
    weighted_one = dnormed * norm_one
    inner_one = feature_total(jnp.sum(weighted_one * token_vals, axis=1)) / D
    grad_input = (
        dresid
        + scale_one[:, None] * weighted_one
        - token_vals * (scale_one**3 * inner_one)[:, None]
    )
    grad_norm_one = jnp.sum(dnormed * token_vals * scale_one[:, None], axis=0)
    grad_sums = (
        lax.psum(grad_wq.astype(jnp.bfloat16), "dp").astype(jnp.float32),
        lax.psum(grad_wk.astype(jnp.bfloat16), "dp").astype(jnp.float32),
        lax.psum(grad_wv.astype(jnp.bfloat16), "dp").astype(jnp.float32),
        lax.psum(grad_wo.astype(jnp.bfloat16), "dp").astype(jnp.float32),
        lax.psum(grad_gate.astype(jnp.bfloat16), "dp").astype(jnp.float32),
        lax.psum(grad_up.astype(jnp.bfloat16), "dp").astype(jnp.float32),
        lax.psum(grad_down.astype(jnp.bfloat16), "dp").astype(jnp.float32),
    )
    gain_sums = lax.psum((grad_norm_one, grad_norm_two), ("dp", "col"))
    return (
        output,
        grad_input,
        gain_sums[0],
        grad_sums[0],
        grad_sums[1],
        grad_sums[2],
        grad_sums[3],
        gain_sums[1],
        grad_sums[4],
        grad_sums[5],
        grad_sums[6],
    )


def solution(mesh):
    in_specs = (
        P(("dp", "col"), "row"),
        P(("dp", "col"), "row"),
        P("dp", None),
        P("row"),
        P("row", "col"),
        P("row", "col"),
        P("row", "col"),
        P("col", "row"),
        P("row"),
        P("row", "col"),
        P("row", "col"),
        P("col", "row"),
    )
    out_specs = (
        P(("dp", "col"), "row"),
        P(("dp", "col"), "row"),
        P("row"),
        P("row", "col"),
        P("row", "col"),
        P("row", "col"),
        P("col", "row"),
        P("row"),
        P("row", "col"),
        P("row", "col"),
        P("col", "row"),
    )
    return jax.shard_map(
        per_device, mesh=mesh, in_specs=in_specs, out_specs=out_specs, check_vma=False
    )
```

profile of v0, /device:TPU:0, one launch (start us, length us, event | category | flops | bytes accessed | tf_op | source)
XLA Modules:
  0.0 615.0 jit_solution(9189590922999881317)
XLA Ops:
  7.2 1.2 fusion.23
  8.4 8.3 %psum.91 = f32[512]{0:T(512)S(1)} all-reduce(f32[512]{0:T(512)S(1)} %fusion.23), channel_id=1, replica_groups=mesh['dp'=4,'row'=4,'col'=2] {'row'}, use_global_device_ids=true, to_apply=%region_1.0 | all-reduce | flops 512 | bytes 4096 | tf_op jit(solution)/shard_map/psum | solution.py:65
  16.8 1.1 fusion.25
  17.8 7.4 %all_gather.24 = bf16[1024,256]{1,0:T(8,128)(2,1)S(1)} all-gather(bf16[512,256]{1,0:T(8,128)(2,1)S(1)} %fusion.25), channel_id=1, replica_groups=mesh['dp'=4,'row'=4,'col'=2] {'col'}, dimensions={0}, use_global_device_ids=true | all-gather | bytes 786432 | tf_op jit(solution)/shard_map/all_gather | solution.py:45
  29.0 2.6 convolution_convert_fusion.3
  31.7 39.5 %reduce-scatter.9.cloned.1.call-done = bf16[256,1536]{1,0:T(8,128)(2,1)} async-done(((bf16[1024,1536]{1,0:T(8,128)(2,1)}), bf16[256,1536]{1,0:T(8,128)(2,1)}) %reduce-scatter.9.cloned.1.call-update) | async-done | bytes 786448 | tf_op jit(solution)/shard_map/reduce_scatter | solution.py:53
  71.2 1.1 slice.64
  72.3 1.8 collective-permute-start
  76.6 1.3 copy.33
  77.8 1.3 copy.31
  80.0 1.3 exponential_reduce_fusion
  81.4 1.9 convolution_convert_fusion.12
  83.4 24.2 %all-gather.5.cloned.1.call-done = bf16[1024,512]{0,1:T(8,128)(2,1)} async-done(((bf16[256,512]{0,1:T(8,128)(2,1)}), bf16[1024,512]{0,1:T(8,128)(2,1)}) %all-gather.5.cloned.1.call-update) | async-done | bytes 1048592 | tf_op jit(solution)/shard_map/all_gather | solution.py:49
  107.5 2.5 convolution_convert_fusion.7
  111.0 2.0 constant_dynamic-update-slice_fusion.3
  113.1 12.0 %reduce-scatter.11.cloned.1.call-done = bf16[512,256]{1,0:T(8,128)(2,1)} async-done(((bf16[1024,256]{1,0:T(8,128)(2,1)}), bf16[512,256]{1,0:T(8,128)(2,1)}) %reduce-scatter.11.cloned.1.call-update) | async-done | bytes 262160 | tf_op jit(solution)/shard_map/reduce_scatter | solution.py:59
  125.0 1.1 multiply_reduce_fusion.1
  126.1 6.9 %psum.92 = f32[512]{0:T(512)S(1)} all-reduce(f32[512]{0:T(512)S(1)} %multiply_reduce_fusion.1), channel_id=1, replica_groups=mesh['dp'=4,'row'=4,'col'=2] {'row'}, use_global_device_ids=true, to_apply=%region_7.8 | all-reduce | flops 512 | bytes 4096 | tf_op jit(solution)/shard_map/psum | solution.py:65
  133.0 1.1 multiply_convert_fusion.2
  134.1 7.6 %all_gather.26 = bf16[1024,256]{1,0:T(8,128)(2,1)S(1)} all-gather(bf16[512,256]{1,0:T(8,128)(2,1)S(1)} %multiply_convert_fusion.2), channel_id=1, replica_groups=mesh['dp'=4,'row'=4,'col'=2] {'col'}, dimensions={0}, use_global_device_ids=true | all-gather | bytes 786432 | tf_op jit(solution)/shard_map/all_gather | solution.py:45
  141.7 5.5 convolution_convert_fusion
  148.1 7.0 %all_gather.28 = bf16[1024,256]{1,0:T(8,128)(2,1)S(1)} all-gather(bf16[512,256]{1,0:T(8,128)(2,1)S(1)} %copy-done.5), channel_id=1, replica_groups=mesh['dp'=4,'row'=4,'col'=2] {'col'}, dimensions={0}, use_global_device_ids=true | all-gather | bytes 786432 | tf_op jit(solution)/shard_map/all_gather | solution.py:45
  155.9 2.6 convolution_convert_fusion.2
  158.6 43.7 %reduce-scatter.13.cloned.1.call-done = bf16[256,2816]{1,0:T(8,128)(2,1)} async-done(((bf16[1024,2816]{1,0:T(8,128)(2,1)}), bf16[256,2816]{1,0:T(8,128)(2,1)}) %reduce-scatter.13.cloned.1.call-update) | async-done | bytes 1441808 | tf_op jit(solution)/shard_map/reduce_scatter | solution.py:53
  202.3 3.1 convert_element_type.142
  205.4 35.8 %reduce-scatter.17.cloned.1.call-done = bf16[256,1408]{1,0:T(8,128)(2,1)} async-done(((bf16[1024,1408]{1,0:T(8,128)(2,1)}), bf16[256,1408]{1,0:T(8,128)(2,1)}) %reduce-scatter.17.cloned.1.call-update) | async-done | bytes 720912 | tf_op jit(solution)/shard_map/reduce_scatter | solution.py:53
  241.2 3.7 fusion.4
  244.9 1.2 pad_maximum_fusion
  246.4 43.3 %all-gather.9.cloned.1.call-done = bf16[1024,2816]{1,0:T(8,128)(2,1)} async-done(((bf16[256,2816]{1,0:T(8,128)(2,1)}), bf16[1024,2816]{1,0:T(8,128)(2,1)}) %all-gather.9.cloned.1.call-update) | async-done | bytes 5767184 | tf_op jit(solution)/shard_map/all_gather | solution.py:49
  289.7 5.5 convolution_convert_fusion.10
  295.3 14.7 %reduce-scatter.19.cloned.1.call-done = bf16[512,256]{1,0:T(8,128)(2,1)} async-done(((bf16[1024,256]{1,0:T(8,128)(2,1)}), bf16[512,256]{1,0:T(8,128)(2,1)}) %reduce-scatter.19.cloned.1.call-update) | async-done | bytes 262160 | tf_op jit(solution)/shard_map/reduce_scatter | solution.py:59
  310.0 1.2 fusion.21
  311.2 6.9 %psum.93 = f32[512]{0:T(512)S(1)} all-reduce(f32[512]{0:T(512)S(1)} %get-tuple-element.46), channel_id=1, replica_groups=mesh['dp'=4,'row'=4,'col'=2] {'row'}, use_global_device_ids=true, to_apply=%region_13.14 | all-reduce | flops 512 | bytes 4096 | tf_op jit(solution)/shard_map/psum | solution.py:65
  318.1 1.2 fusion.35
  319.3 7.5 %all_gather.30 = bf16[1024,256]{1,0:T(8,128)(2,1)S(1)} all-gather(bf16[512,256]{1,0:T(8,128)(2,1)S(1)} %fusion.35), channel_id=1, replica_groups=mesh['dp'=4,'row'=4,'col'=2] {'col'}, dimensions={0}, use_global_device_ids=true | all-gather | bytes 786432 | tf_op jit(solution)/shard_map/all_gather | solution.py:45
  327.7 2.4 convolution_convert_fusion.6
  330.1 25.0 %reduce-scatter.21.cloned.1.call-done = bf16[256,512]{1,0:T(8,128)(2,1)} async-done(((bf16[1024,512]{1,0:T(8,128)(2,1)}), bf16[256,512]{1,0:T(8,128)(2,1)}) %reduce-scatter.21.cloned.1.call-update) | async-done | bytes 262160 | tf_op jit(solution)/shard_map/reduce_scatter | solution.py:53
  355.2 1.8 copy.34
  357.0 3.6 fusion.32
  360.7 1.8 multiply_reduce_fusion
  362.5 1.2 multiply_convert_fusion
  364.3 1.3 collective-permute-start.1
  366.4 1.7 collective-permute-done.1
  369.9 34.6 %all-gather.11.cloned.1.call-done = bf16[1024,1536]{0,1:T(8,128)(2,1)} async-done(((bf16[256,1536]{0,1:T(8,128)(2,1)}), bf16[1024,1536]{0,1:T(8,128)(2,1)}) %all-gather.11.cloned.1.call-update) | async-done | bytes 3145744 | tf_op jit(solution)/shard_map/all_gather | solution.py:49
  404.5 3.9 convolution_convert_fusion.9
  408.5 24.5 %all-gather.7.cloned.1.call-done = bf16[1024,1408]{1,0:T(8,128)(2,1)} async-done(((bf16[256,1408]{1,0:T(8,128)(2,1)}), bf16[1024,1408]{1,0:T(8,128)(2,1)}) %all-gather.7.cloned.1.call-update) | async-done | bytes 2883600 | tf_op jit(solution)/shard_map/all_gather | solution.py:49
  433.0 3.6 convolution_convert_fusion.8
  436.9 3.6 convolution_convert_fusion.4
  440.6 4.6 convolution_convert_fusion.1
  445.2 1.2 fusion.36
  446.4 1.1 convolution_convert_fusion.11
  447.6 1.1 convolution_convert_fusion.5
  450.4 1.2 fusion.28
  451.7 21.3 %all-reduce.1 = (f32[256]{0:T(256)}, f32[256]{0:T(256)}) all-reduce(f32[256]{0:T(256)S(1)} %get-tuple-element.47, f32[256]{0:T(256)S(1)} %get-tuple-element.45), channel_id=1, replica_groups=mesh['dp'=4,'row'=4,'col'=2] {'dp','col'}, use_global_device_ids=true, to_apply=%region_20.21 | all-reduce | flops 512 | bytes 4096 | tf_op jit(solution)/shard_map/psum | solution.py:272
  472.9 5.6 psum.94
  478.6 2.3 fusion.16
  480.9 116.6 %all-reduce.5.cloned.1.call-done = (bf16[256,512]{1,0:T(8,128)(2,1)}, bf16[256,512]{1,0:T(8,128)(2,1)}, bf16[256,512]{1,0:T(8,128)(2,1)}, bf16[512,256]{1,0:T(8,...) async-done(((bf16[256,512]{1,0:T(8,128)(2,1)}, bf16[256,512]{1,0:T(8,128)(2,1)}, bf16[256,512]{1,0:T(8,128)(2,1)}, ...) | async-done | bytes 3211280 | tf_op jit(solution)/shard_map/psum | solution.py:264
  597.5 1.9 convert_element_type.160
  599.4 1.8 convert_element_type.161
  601.2 1.9 convert_element_type.162
  603.1 1.8 convert_element_type.164
  604.9 1.2 convert_element_type.165
  606.1 1.2 convert_element_type.166
  607.3 1.2 convert_element_type.168
  (101 shorter events, 16.7 us)
Async XLA Ops:
  7.2 148.8 %copy-start = (bf16[1408,256]{1,0:T(8,128)(2,1)S(1)}, bf16[1408,256]{1,0:T(8,128)(2,1)}, u32[]{:S(2)}) copy-start(bf16[1408,256]{1,0:T(8,128)(2,1)} %param.23) | copy-start | bytes 2162692
  7.2 64.0 %reduce-scatter.9.cloned.1.call-start = ((), (), s32[]{:S(2)}) async-start(), calls=%async_computation.8 | async-start | bytes 3932160 | tf_op jit(solution)/shard_map/reduce_scatter | solution.py:53
  28.2 0.9 copy-start.13
  31.6 42.4 %copy-start.20 = (s32[1,1024]{1,0:T(1,128)S(1)}, s32[1,1024]{1,0:T(1,128)}, u32[]{:S(2)}) copy-start(s32[1,1024]{1,0:T(1,128)} %param.14) | copy-start | bytes 12292
  31.7 75.9 %all-gather.5.cloned.1.call-start = ((), (), s32[]{:S(2)}) async-start(), calls=%async_computation.9 | async-start | bytes 1310720 | tf_op jit(solution)/shard_map/all_gather | solution.py:49
  72.3 3.3 collective-permute-start
  79.1 2.3 copy-start.7
  80.0 3.3 copy-start.1
  81.4 26.2 %copy-start.19 = (bf16[512,256]{1,0:T(8,128)(2,1)S(1)}, bf16[512,256]{1,0:T(8,128)(2,1)}, u32[]{:S(2)}) copy-start(bf16[512,256]{1,0:T(8,128)(2,1)} %param.19) | copy-start | bytes 786436
  83.3 26.8 %copy-start.15 = (bf16[256,1408]{1,0:T(8,128)(2,1)S(1)}, bf16[256,1408]{1,0:T(8,128)(2,1)}, u32[]{:S(2)}) copy-start(bf16[256,1408]{1,0:T(8,128)(2,1)} %param.21) | copy-start | bytes 2162692
  83.3 41.7 %copy-start.3 = (bf16[512,256]{1,0:T(8,128)(2,1)S(1)}, bf16[512,256]{1,0:T(8,128)(2,1)}, u32[]{:S(2)}) copy-start(bf16[512,256]{1,0:T(8,128)(2,1)} %param.12) | copy-start | bytes 786436
  83.3 49.7 %copy-start.21 = (f32[256]{0:T(256)S(1)}, f32[256]{0:T(256)}, u32[]{:S(2)}) copy-start(f32[256]{0:T(256)} %param.20) | copy-start | bytes 3076
  83.3 41.7 %reduce-scatter.11.cloned.1.call-start = ((), (), s32[]{:S(2)}) async-start(), calls=%async_computation.10 | async-start | bytes 786432 | tf_op jit(solution)/shard_map/reduce_scatter | solution.py:59
  110.1 92.2 %reduce-scatter.13.cloned.1.call-start = ((), (), s32[]{:S(2)}) async-start(), calls=%async_computation.11 | async-start | bytes 7208960 | tf_op jit(solution)/shard_map/reduce_scatter | solution.py:53
  147.2 0.9 copy-start.5
  147.2 94.0 %reduce-scatter.17.cloned.1.call-start = ((), (), s32[]{:S(2)}) async-start(), calls=%async_computation.14 | async-start | bytes 3604480 | tf_op jit(solution)/shard_map/reduce_scatter | solution.py:53
  155.1 0.8 copy-start.11
  158.6 131.2 %all-gather.9.cloned.1.call-start = ((), (), s32[]{:S(2)}) async-start(), calls=%async_computation.15 | async-start | bytes 7208960 | tf_op jit(solution)/shard_map/all_gather | solution.py:49
  246.2 63.8 %copy-start.4 = (bf16[512,256]{1,0:T(8,128)(2,1)S(1)}, bf16[512,256]{1,0:T(8,128)(2,1)}, u32[]{:S(2)}) copy-start(bf16[512,256]{1,0:T(8,128)(2,1)} %reduce-scatter.11.cloned.1.call-done) | copy-start | bytes 786436
  246.2 63.8 %reduce-scatter.19.cloned.1.call-start = ((), (), s32[]{:S(2)}) async-start(), calls=%async_computation.16 | async-start | bytes 786432 | tf_op jit(solution)/shard_map/reduce_scatter | solution.py:59
  295.3 59.9 %reduce-scatter.21.cloned.1.call-start = ((), (), s32[]{:S(2)}) async-start(), calls=%async_computation.17 | async-start | bytes 1310720 | tf_op jit(solution)/shard_map/reduce_scatter | solution.py:53
  326.9 0.8 copy-start.9
  330.1 74.5 %all-gather.11.cloned.1.call-start = ((), (), s32[]{:S(2)}) async-start(), calls=%async_computation.18 | async-start | bytes 3932160 | tf_op jit(solution)/shard_map/all_gather | solution.py:49
  357.0 3.6 copy-start.2
  357.0 3.6 copy-start.8
  357.0 3.7 copy-start.14
  364.3 3.8 collective-permute-start.1
  369.3 63.8 %all-gather.7.cloned.1.call-start = ((), (), s32[]{:S(2)}) async-start(), calls=%async_computation.12 | async-start | bytes 3604480 | tf_op jit(solution)/shard_map/all_gather | solution.py:49
  369.8 80.6 %reduce-scatter.23.cloned.1.call-start = ((), (), s32[]{:S(2)}) async-start(), calls=%async_computation.19 | async-start | bytes 786432 | tf_op jit(solution)/shard_map/reduce_scatter | solution.py:59
  408.5 28.4 %copy-start.12 = (bf16[1024,256]{1,0:T(8,128)(2,1)S(1)}, bf16[1024,256]{1,0:T(8,128)(2,1)}, u32[]{:S(2)}) copy-start(bf16[1024,256]{1,0:T(8,128)(2,1)} %copy-done.11) | copy-start | bytes 1572868
  408.5 70.1 %reduce-scatter.15.cloned.1.call-start = ((), (), s32[]{:S(2)}) async-start(), calls=%async_computation.13 | async-start | bytes 786432 | tf_op jit(solution)/shard_map/reduce_scatter | solution.py:59
  436.6 160.9 %all-reduce.5.cloned.1.call-start = ((), (), s32[]{:S(2)}) async-start(), calls=%async_computation.20 | async-start | bytes 6422528 | tf_op jit(solution)/shard_map/psum | solution.py:264
  440.5 5.8 copy-start.10
  440.5 5.8 copy-start.24
  445.2 2.4 copy-start.23
  448.7 1.8 copy-start.22
  448.7 29.9 %copy-start.6 = (bf16[512,256]{1,0:T(8,128)(2,1)S(1)}, bf16[512,256]{1,0:T(8,128)(2,1)}, u32[]{:S(2)}) copy-start(bf16[512,256]{1,0:T(8,128)(2,1)} %reduce-scatter.19.cloned.1.call-done) | copy-start | bytes 786436
  597.5 7.4 %copy-start.18 = (bf16[256,1408]{1,0:T(8,128)(2,1)S(1)}, bf16[256,1408]{1,0:T(8,128)(2,1)}, u32[]{:S(2)}) copy-start(bf16[256,1408]{1,0:T(8,128)(2,1)} %get-tuple-element.63) | copy-start | bytes 2162692
  597.5 8.6 %copy-start.17 = (bf16[256,1408]{1,0:T(8,128)(2,1)S(1)}, bf16[256,1408]{1,0:T(8,128)(2,1)}, u32[]{:S(2)}) copy-start(bf16[256,1408]{1,0:T(8,128)(2,1)} %get-tuple-element.64) | copy-start | bytes 2162692
  601.2 6.0 copy-start.16
Sparse Core Ops, SparseCore 0:
  31.8 39.3 reduce-scatter.8
  83.4 24.0 all-gather.4
  110.4 14.5 reduce-scatter.10
  147.3 54.9 reduce-scatter.12
  204.8 36.3 reduce-scatter.16
  246.3 43.4 all-gather.8
  295.4 14.5 reduce-scatter.18
  330.2 24.9 reduce-scatter.20
  369.4 35.1 all-gather.10
  405.9 27.0 all-gather.6
  435.8 14.5 reduce-scatter.22
  453.2 14.8 reduce-scatter.14
  472.1 125.3 all-reduce.4
where the time goes:
time: 616 us; the launch traced here: 615 us
  waiting for transfers between devices  417 us (68%)
  blocking collectives  78.5 us (13%)
  matrix products  48.5 us (8%)
  other arithmetic  34.5 us (6%)
  local copies, waits for them, and re-layouts  18.1 us (3%)
  between operations  14.2 us (2%)
    reduce_scatter x4, waiting for transfers between devices, summed_row(): lax.psum_scatter(array_in.astype(jnp.bfloat16), 'row', scatter_dimension=...  144 us
    all_gather x4, waiting for transfers between devices, tokens_row(): lax.all_gather(for_sending(array_in), 'row', axis=0, tiled=True)  127 us
    psum x1, waiting for transfers between devices, per_device(): lax.psum(grad_wq.astype(jnp.bfloat16), 'dp').astype(jnp.float32)  117 us
    all_gather x4, blocking collectives, tokens_col(): return lax.all_gather(array_in, 'col', axis=0, tiled=True)  29.5 us
    psum x4, blocking collectives, feature_total(): return lax.psum(array_in, 'row')  27.7 us
    reduce_scatter x4, waiting for transfers between devices, summed_col(): lax.psum_scatter(array_in.astype(jnp.bfloat16), 'col', scatter_dimension=...  27.5 us
    psum x1, blocking collectives, per_device(): gain_sums = lax.psum((grad_norm_one, grad_norm_two), ('dp', 'col'))  21.3 us
    dot_general x4, matrix products, matmul_nt(): lax.dot_general(first_op, second_op, (((1,), (1,)), ((), ())), preferred_...  14.4 us
  transfers between devices with their start and end apart: 15, of which 13 were waited for; matrix products, arithmetic and copies ran while one was open for 6% of the time, Pallas kernels for 0%

commit v1 on v0

--- a/solution.py
+++ b/solution.py
@@ -1,6 +1,10 @@
+import functools
+
 import jax
 import jax.numpy as jnp
 from jax import lax
+from jax.experimental import pallas as pl
+from jax.experimental.pallas import tpu as pltpu
 from jax.sharding import PartitionSpec as P
 
 D = 1024
@@ -285,6 +289,678 @@
     )
 
 
+MESH = pl.DeviceIdType.MESH
+BF = jnp.bfloat16
+F32 = jnp.float32
+NPLANE = 8
+
+
+def contract(a, b, ca, cb):
+    return lax.dot_general(a, b, (((ca,), (cb,)), ((), ())), preferred_element_type=F32)
+
+
+class Copies:
+    def __init__(self, send, recv):
+        self.send, self.recv, self.used, self.open = send, recv, 0, []
+
+    def take(self, amount=1):
+        base = self.used
+        self.used += amount
+        return base
+
+    def make(self, src, dst, to, site=None):
+        site = self.take() if site is None else site
+        return pltpu.make_async_remote_copy(
+            src_ref=src,
+            dst_ref=dst,
+            send_sem=self.send.at[site],
+            recv_sem=self.recv.at[site],
+            device_id=to,
+            device_id_type=MESH,
+        )
+
+    def start(self, copy, when=None):
+        self.open.append((copy, when))
+        if when is None:
+            copy.start()
+        else:
+            pl.when(when)(copy.start)
+
+    def finish(self):
+        for copy, when in self.open:
+            if when is None:
+                copy.wait_send()
+            else:
+                pl.when(when)(copy.wait_send)
+        self.open = []
+
+
+def layer_kernel(nz, ff_half, ff_cut, *refs):
+    it = iter(refs)
+    take = lambda n: [next(it) for _ in range(n)]
+    tok, cot, seg, n1, wq, wk, wv, wo, n2, wg, wu, wd = take(12)
+    out, gin, gn1, gwq, gwk, gwv, gwo, gn2, gwg, gwu, gwd = take(11)
+    X, G, WQKV, WO, WG, WU, WD, NG1, NG2 = take(9)
+    XN, Q, K, V, BIAS, PM, A = take(7)
+    PART, RY, RX, SX = take(4)
+    HN, RES, DRES, ACT, DGA, DUP, DB, DAT = take(8)
+    DK, DV, DQKV, HS, HR = take(5)
+    OS, GS, GP, GR, GZ, GZS = take(6)
+    zbufs = [take(5) for _ in range(5)]
+    OFQ, OFO, OFF1, OFF2, OFD = take(5)
+    send, recv, loc = take(3)
+
+    z, row, y = lax.axis_index("dp"), lax.axis_index("row"), lax.axis_index("col")
+    x, c = row // 2, row % 2
+    net = Copies(send, recv)
+    nloc = [0]
+
+    def local(src, dst):
+        nloc[0] += 1
+        return pltpu.make_async_copy(src, dst, loc.at[nloc[0] - 1])
+
+    def dev(zz, xx, yy, cc):
+        return (zz, 2 * xx + cc, yy)
+
+    core_nb, x_nb, y_nb = dev(z, x, y, 1 - c), dev(z, 1 - x, y, c), dev(z, x, 1 - y, c)
+    z_up, z_dn = dev(z + 1, x, y, c), dev(z - 1, x, y, c)
+    lanes = lambda i, n=256: pl.ds(pl.multiple_of(i * n, 128), n)
+    rows = lambda i, n: pl.ds(pl.multiple_of(i * n, n if n % 16 else 16), n)
+    flip = lambda v, bit: 1 - v if bit else v
+
+    barrier = pltpu.get_barrier_semaphore()
+    for d in range(1, NPLANE):
+        pl.semaphore_signal(
+            barrier, inc=1, device_id=dev(z, flip(x, d & 1), flip(y, d & 2), flip(c, d & 4)), device_id_type=MESH
+        )
+    for d in range(1, nz):
+        pl.semaphore_signal(barrier, inc=1, device_id=dev((z + d) % nz, x, y, c), device_id_type=MESH)
+    pl.semaphore_wait(barrier, NPLANE - 1 + nz - 1)
+
+    def gather_tokens(src, buf):
+        col = lambda rr: buf.at[:, lanes(rr)]
+        mine = c == y
+        keep = local(src, col(row))
+        pl.when(mine)(keep.start)
+        over = net.make(src, col(row), core_nb)
+        bx, by, bf = net.take(2), net.take(2), net.take(2)
+        net.start(net.make(src, col(row), dev(z, 1 - x, y, y), bx + c))
+        net.start(net.make(src, col(row), dev(z, x, 1 - y, y), by + c))
+        net.start(over, jnp.logical_not(mine))
+        fw = [net.make(col(2 * (1 - x) + k), col(2 * (1 - x) + k), y_nb, bf + k) for k in range(2)]
+        inx = [net.make(src, col(row), core_nb, bx + k) for k in range(2)]
+        iny = [net.make(src, col(row), core_nb, by + k) for k in range(2)]
+
+        def arrive():
+            @pl.when(mine)
+            def _():
+                for k in range(2):
+                    inx[k].wait_recv()
+                    fw[k].start()
+                over.wait_recv()
+                keep.wait()
+
+            net.open += [(f, mine) for f in fw]
+
+        def rest():
+            @pl.when(jnp.logical_not(mine))
+            def _():
+                for k in range(2):
+                    iny[k].wait_recv()
+                for k in range(2):
+                    fw[k].wait_recv()
+
+        return arrive, rest
+
+    def relay(src_of, dst_of):
+        keep = local(src_of(x), dst_of(row))
+        across = net.make(src_of(x), dst_of(row), core_nb)
+        far = net.make(src_of(1 - x), dst_of(row), x_nb)
+        theirs = dst_of(2 * (1 - x) + c)
+        fwd = net.make(theirs, theirs, core_nb)
+
+        def start():
+            keep.start()
+            net.start(far)
+            net.start(across)
+
+        def arrive():
+            far.wait_recv()
+            net.start(fwd)
+
+        def rest():
+            keep.wait()
+            across.wait_recv()
+            fwd.wait_recv()
+
+        return start, arrive, rest
+
+    def gather_gain(src, dst):
+        keep = local(src, dst.at[:, lanes(row)])
+        keep.start()
+        got = []
+        for to in (core_nb, x_nb, dev(z, 1 - x, y, 1 - c)):
+            got.append(net.make(src, dst.at[:, lanes(row)], to))
+            net.start(got[-1])
+
+        def rest():
+            keep.wait()
+            for g in got:
+                g.wait_recv()
+
+        return rest
+
+    gx = gather_tokens(tok, X)
+    rq = [
+        relay(
+            lambda xx, w=w: w.at[:, lanes(xx)],
+            lambda rr, i=i: WQKV.at[rows(rr, 256), pl.ds(i * 256, 256)],
+        )
+        for i, w in enumerate((wq, wk, wv))
+    ]
+    for r in rq:
+        r[0]()
+    ga = [gather_gain(n1, NG1), gather_gain(n2, NG2)]
+    gx[0]()
+    gg = gather_tokens(cot, G)
+    ro = relay(lambda xx: wo.at[rows(xx, 256), :], lambda rr: WO.at[:, lanes(rr)])
+    rg = relay(lambda xx: wg.at[:, pl.ds(pl.multiple_of(xx * ff_cut, 128), ff_half)], lambda rr: WG.at[rows(rr, 256), :])
+    ru = relay(lambda xx: wu.at[:, pl.ds(pl.multiple_of(xx * ff_cut, 128), ff_half)], lambda rr: WU.at[rows(rr, 256), :])
+    rd = relay(lambda xx: wd.at[pl.ds(pl.multiple_of(xx * ff_cut, 128), ff_half), :], lambda rr: WD.at[:, lanes(rr)])
+    for r in rq:
+        r[1]()
+    for r in (ro, rg, ru, rd):
+        r[0]()
+    for _, _, ZR, _, _ in zbufs:
+
+        @pl.when(z == 0)
+        def _(ZR=ZR):
+            ZR[0, nz - 2] = jnp.zeros(ZR.shape[2:], BF)
+
+        @pl.when(z == nz - 1)
+        def _(ZR=ZR):
+            ZR[1, nz - 2] = jnp.zeros(ZR.shape[2:], BF)
+
+    seg_f = seg[...].astype(F32)
+    own = jnp.where(c == 0, seg_f[:, :512], seg_f[:, 512:])
+    before = jnp.where(c == 0, jnp.full((1, 256), -1.0, F32), seg_f[:, 256:512])
+    ids = jnp.concatenate([before, own], axis=1)
+    for b in range(2):
+        k_id = jnp.broadcast_to(ids[:, b * 256 : b * 256 + 512], (256, 512))
+        q_id = jnp.broadcast_to(ids[:, 256 + b * 256 : 512 + b * 256], (512, 256)).T
+        q_pos = lax.broadcasted_iota(jnp.int32, (256, 512), 0) + 256
+        k_pos = lax.broadcasted_iota(jnp.int32, (256, 512), 1)
+        BIAS[b] = jnp.where((q_id == k_id) & (k_pos <= q_pos), 0.0, NEGATIVE)
+
+    @pl.when(c == 0)
+    def _():
+        K[0:256, :] = jnp.zeros((256, 256), BF)
+        V[0:256, :] = jnp.zeros((256, 256), BF)
+
+    for g in ga:
+        g()
+    gx[1]()
+    for t in range(4):
+        v = X[t * 128 : t * 128 + 128, :].astype(F32)
+        scale = lax.rsqrt(jnp.mean(v * v, axis=1, keepdims=True) + EPSILON)
+        XN[t * 128 : t * 128 + 128, :] = (v * scale * NG1[...]).astype(BF)
+    for r in rq:
+        r[2]()
+    K[256:768, :] = contract(XN[...], WQKV[:, 256:512], 1, 0).astype(BF)
+    V[256:768, :] = contract(XN[...], WQKV[:, 512:768], 1, 0).astype(BF)
+    hk = net.make(K.at[pl.ds(512, 256), :], K.at[pl.ds(0, 256), :], core_nb)
+    hv = net.make(V.at[pl.ds(512, 256), :], V.at[pl.ds(0, 256), :], core_nb)
+    net.start(hk, c == 0)
+    net.start(hv, c == 0)
+    Q[...] = (contract(XN[...], WQKV[:, 0:256], 1, 0).astype(BF) * 0.125).astype(BF)
+
+    gg[0]()
+    @pl.when(c == 1)
+    def _():
+        hk.wait_recv()
+        hv.wait_recv()
+
+    lane_id = lax.broadcasted_iota(jnp.int32, (1, 128), 1)
+    head_mask = [jnp.where(lane_id < 64, 1.0, 0.0).astype(BF), jnp.where(lane_id < 64, 0.0, 1.0).astype(BF)]
+
+    def attend(b, carry):
+        for hp in range(2):
+            cols = slice(hp * 128, hp * 128 + 128)
+            q_b = Q[pl.ds(pl.multiple_of(b * 256, 256), 256), cols]
+            k_b = K[pl.ds(pl.multiple_of(b * 256, 256), 512), cols]
+            v_b = V[pl.ds(pl.multiple_of(b * 256, 256), 512), cols]
+            total = None
+            for h in range(2):
+                s = contract(q_b * head_mask[h], k_b, 1, 1) + BIAS[b]
+                e = jnp.exp(s - jnp.max(s, axis=1, keepdims=True))
+                p = e * (1.0 / jnp.sum(e, axis=1, keepdims=True))
+                PM[b * 4 + hp * 2 + h] = p
+                part = contract(p.astype(BF), v_b * head_mask[h], 1, 0)
+                total = part if total is None else total + part
+            A[pl.ds(pl.multiple_of(b * 256, 256), 256), cols] = total.astype(BF)
+        return carry
+
+    lax.fori_loop(0, 2, attend, 0)
+    for r in (ro, rg, ru, rd):
+        r[1]()
+
+    j = 2 * x + y
+    shard = lambda buf, jj: buf.at[rows(jj, 128), :]
+
+    def reduce_start(k, p):
+        part = PART.at[p]
+        a = net.make(shard(part, 2 * (1 - x) + 1 - y), RY.at[k, 0], y_nb)
+        b = net.make(shard(part, 2 * x + 1 - y), RY.at[k, 1], y_nb)
+        d = net.make(SX.at[k], RX.at[k], x_nb)
+        a.start()
+        b.start()
+
+        def mid():
+            a.wait_recv()
+            SX[k] = (PART[p, rows(2 * (1 - x) + y, 128), :].astype(F32) + RY[k, 0].astype(F32)).astype(BF)
+            d.start()
+
+        def end():
+            b.wait_recv()
+            d.wait_recv()
+            for copy in (a, b, d):
+                copy.wait_send()
+            return PART[p, rows(j, 128), :].astype(F32) + RY[k, 1].astype(F32) + RX[k].astype(F32)
+
+        return mid, end
+
+    def gather_start(buf):
+        a = net.make(shard(buf, j), shard(buf, j), x_nb)
+        b = net.make(shard(buf, j), shard(buf, j), y_nb)
+        jx = 2 * (1 - x) + y
+        f = net.make(shard(buf, jx), shard(buf, jx), y_nb)
+        net.start(a)
+        net.start(b)
+
+        def mid():
+            a.wait_recv()
+            net.start(f)
+
+        def end():
+            b.wait_recv()
+            f.wait_recv()
+
+        return mid, end
+
+    def send_blocks(src, dst):
+        base_r = net.take(4)
+        waits = []
+        for dx in range(2):
+            for cc in range(2):
+                xx = flip(x, dx)
+                piece, place = src.at[:, lanes(2 * xx + cc)], dst.at[rows(j, 128), :]
+                s = net.take()
+                copy = pltpu.make_async_remote_copy(
+                    src_ref=piece,
+                    dst_ref=place,
+                    send_sem=net.send.at[s],
+                    recv_sem=net.recv.at[base_r + dx * 2 + y],
+                    device_id=dev(z, xx, c, cc),
+                    device_id_type=MESH,
+                )
+                if dx == 0:
+                    here = (c == y) & (c == cc)
+                    keep = local(piece, place)
+                    pl.when(here)(keep.start)
+                    net.start(copy, jnp.logical_not(here))
+                    waits.append((keep, here))
+                else:
+                    net.start(copy)
+        piece, place = src.at[:, pl.ds(0, 256)], dst.at[pl.ds(0, 128), :]
+        arrivals = [
+            (net.make(piece, place, core_nb, base_r + dx * 2 + yy), jnp.logical_not((c == y) & (y == yy)) if dx == 0 else None)
+            for dx in range(2)
+            for yy in range(2)
+        ]
+
+        def end():
+            for keep, here in waits:
+                pl.when(here)(keep.wait)
+            for got, when in arrivals:
+                if when is None:
+                    got.wait_recv()
+                else:
+                    pl.when(when)(got.wait_recv)
+
+        return end
+
+    def along_z(bufs, deliver):
+        GB, CR, ZR, RL, FF = bufs
+        n_rows = CR.shape[1] // nz
+        part = lambda q: CR.at[:, rows(q, n_rows), :]
+        over = net.make(GB.at[1 - c], CR, core_nb)
+        ends = []
+        net.start(over)
+        yield
+        over.wait_recv()
+        for xx in range(2):
+            CR[xx] = (CR[xx].astype(F32) + GB[c, xx].astype(F32)).astype(BF)
+        up = [net.take() for _ in range(nz - 1)]
+        dn = [net.take() for _ in range(nz - 1)]
+        for s in range(1, nz):
+            for way, sites, to in ((0, up, z_up), (1, dn, z_dn)):
+                zz = z if way == 0 else nz - 1 - z
+                q = nz - s + zz
+                q = q if way == 0 else nz - 1 - q
+                go = (zz < nz - 1) & (zz <= s - 1)
+                first, later = go & (zz == 0), go & (zz > 0)
+                net.start(net.make(part(q), ZR.at[way, s - 1], to, sites[s - 1]), first)
+                if s >= 2:
+                    acc = ZR.at[way, s - 2]
+                    got = net.make(acc, acc, to, sites[s - 2])
+
+                    @pl.when(later)
+                    def _(got=got, acc=acc, q=q):
+                        got.wait_recv()
+                        acc[...] = (acc[...].astype(F32) + CR[:, rows(q, n_rows), :].astype(F32)).astype(BF)
+
+                    net.start(net.make(acc, ZR.at[way, s - 1], to, sites[s - 1]), later)
+            yield
+        for way, sites in ((0, up), (1, dn)):
+            zz = z if way == 0 else nz - 1 - z
+            last = ZR.at[way, nz - 2]
+            pl.when(zz > 0)(net.make(last, last, z_up, sites[nz - 2]).wait_recv)
+        total = lambda xx: (
+            CR[xx, rows(z, n_rows), :].astype(F32) + ZR[0, nz - 2, xx].astype(F32) + ZR[1, nz - 2, xx].astype(F32)
+        ).astype(BF)
+        RL[...] = total(1 - x)
+        side = net.make(RL, FF.at[z, x], x_nb)
+        net.start(side)
+        FF[z, x] = total(x)
+        yield
+        side.wait_recv()
+        up = [net.take() for _ in range(nz - 1)]
+        dn = [net.take() for _ in range(nz - 1)]
+        net.start(net.make(FF.at[z], FF.at[z], z_up, up[0]), z < nz - 1)
+        net.start(net.make(FF.at[z], FF.at[z], z_dn, dn[0]), z > 0)
+        yield
+        for s in range(2, nz + 1):
+            for way, sites, to in ((0, up, z_up), (1, dn, z_dn)):
+                zz = z if way == 0 else nz - 1 - z
+                q = z - (s - 1) if way == 0 else z + (s - 1)
+                have = zz >= s - 1
+                got = net.make(FF.at[q], FF.at[q], to, sites[s - 2])
+                pl.when(have)(got.wait_recv)
+                if s < nz:
+                    net.start(net.make(FF.at[q], FF.at[q], to, sites[s - 1]), have & (zz < nz - 1))
+            yield
+        deliver(FF)
+        yield
+
+    def flush(buf, dst):
+        copy = local(buf, dst)
+        copy.start()
+        flushes.append(copy)
+
+    flushes = []
+    over_cut = ff_half - ff_cut
+
+    def deliver_qkv(FF):
+        for i, dst in enumerate((gwq, gwk, gwv)):
+            for q in range(nz):
+                for xx in range(2):
+                    OFQ[i, q * 64 : q * 64 + 64, xx * 256 : xx * 256 + 256] = FF[q, xx, :, i * 256 : i * 256 + 256].astype(F32)
+            flush(OFQ.at[i], dst)
+
+    def deliver_wo(FF):
+        for q in range(nz):
+            for xx in range(2):
+                OFO[xx * 256 + q * 64 : xx * 256 + q * 64 + 64, :] = FF[q, xx].astype(F32)
+        flush(OFO, gwo)
+
+    def deliver_pair(buf, dst):
+        def run(FF):
+            for q in range(nz):
+                buf[q * 64 : q * 64 + 64, 0:ff_half] = FF[q, 0].astype(F32)
+                buf[q * 64 : q * 64 + 64, ff_half:] = FF[q, 1, :, over_cut:].astype(F32)
+            flush(buf, dst)
+
+        return run
+
+    def deliver_down(FF):
+        n = ff_half // nz
+        for q in range(nz):
+            OFD[q * n : q * n + n, :] = FF[q, 0].astype(F32)
+            skip = max(0, min(n, over_cut - q * n))
+            if skip < n:
+                OFD[ff_cut + q * n + skip : ff_cut + q * n + n, :] = FF[q, 1, skip:, :].astype(F32)
+        flush(OFD, gwd)
+
+    lines = []
+
+    def tick(n=1):
+        for _ in range(n):
+            for line in lines:
+                next(line, None)
+
+    ro[2]()
+    for n in range(4):
+        PART[0, :, n * 256 : n * 256 + 256] = contract(A[...], WO[:, n * 256 : n * 256 + 256], 1, 0).astype(BF)
+    mid, end = reduce_start(0, 0)
+    mid()
+    gg[1]()
+    res = X[rows(j, 128), :].astype(F32) + end()
+    RES[...] = res
+    scale = lax.rsqrt(jnp.mean(res * res, axis=1, keepdims=True) + EPSILON)
+    HN[rows(j, 128), :] = (res * scale * NG2[...]).astype(BF)
+    mid, end = gather_start(HN)
+    mid()
+    for r in (rg, ru, rd):
+        r[2]()
+    end()
+
+    skip = (lax.broadcasted_iota(jnp.int32, (1, 256), 1) < over_cut) & (x == 1)
+    for n in range(ff_half // 256):
+        cols = slice(n * 256, n * 256 + 256)
+        gate = contract(HN[...], WG[:, cols], 1, 0)
+        up = contract(HN[...], WU[:, cols], 1, 0)
+        dact = contract(G[...], WD[cols, :], 1, 1)
+        sig = jax.nn.sigmoid(gate)
+        silu = gate * sig
+        act, dgate, dup = silu * up, dact * up * sig * (1.0 + gate * (1.0 - sig)), dact * silu
+        if n == 0:
+            act, dgate, dup = (jnp.where(skip, 0.0, v) for v in (act, dgate, dup))
+        ACT[:, cols] = act.astype(BF)
+        DGA[:, cols] = dgate.astype(BF)
+        DUP[:, cols] = dup.astype(BF)
+    for n in range(4):
+        cols = slice(n * 256, n * 256 + 256)
+        PART[1, :, cols] = (contract(DGA[...], WG[cols, :], 1, 1) + contract(DUP[...], WU[cols, :], 1, 1)).astype(BF)
+    hid = reduce_start(1, 1)
+    for r in range(4):
+        zbufs[0][0][r % 2, r // 2] = contract(ACT[...], G[:, r * 256 : r * 256 + 256], 0, 0).astype(BF)
+    lines.append(along_z(zbufs[0], deliver_down))
+    tick()
+    for n in range(4):
+        cols = slice(n * 256, n * 256 + 256)
+        PART[2, :, cols] = contract(ACT[...], WD[:, cols], 1, 0).astype(BF)
+    hid[0]()
+    fin = reduce_start(2, 2)
+    tick()
+    for r in range(4):
+        zbufs[1][0][r % 2, r // 2] = contract(HN[:, r * 256 : r * 256 + 256], DGA[...], 0, 0).astype(BF)
+    lines.append(along_z(zbufs[1], deliver_pair(OFF1, gwg)))
+    dh = hid[1]()
+    res = RES[...]
+    scale = lax.rsqrt(jnp.mean(res * res, axis=1, keepdims=True) + EPSILON)
+    w = dh * NG2[...]
+    inner = jnp.mean(w * res, axis=1, keepdims=True)
+    dres = G[rows(j, 128), :].astype(F32) + scale * w - res * (scale * scale * scale * inner)
+    DRES[...] = dres
+    GP[...] = jnp.zeros_like(GP)
+    GP[1:2, :] = jnp.sum(dh * res * scale, axis=0, keepdims=True)
+    DB[rows(j, 128), :] = dres.astype(BF)
+    dbg = gather_start(DB)
+    tick()
+    for r in range(4):
+        zbufs[2][0][r % 2, r // 2] = contract(HN[:, r * 256 : r * 256 + 256], DUP[...], 0, 0).astype(BF)
+    dbg[0]()
+    lines.append(along_z(zbufs[2], deliver_pair(OFF2, gwu)))
+    tick()
+    fin[0]()
+    OS[...] = (RES[...] + fin[1]()).astype(BF)
+    sent = send_blocks(OS, out)
+    dbg[1]()
+
+    DAT[...] = contract(DB[...], WO[...], 1, 1).astype(BF)
+    for r in range(4):
+        zbufs[3][0][r % 2, r // 2] = contract(A[...], DB[:, r * 256 : r * 256 + 256], 0, 0).astype(BF)
+    tick()
+    DK[...] = jnp.zeros_like(DK)
+    DV[...] = jnp.zeros_like(DV)
+
+    def attend_back(b, carry):
+        qs, ks = pl.ds(pl.multiple_of(b * 256, 256), 256), pl.ds(pl.multiple_of(b * 256, 256), 512)
+        for hp in range(2):
+            cols = slice(hp * 128, hp * 128 + 128)
+            q_b, k_b, v_b, d_b = Q[qs, cols], K[ks, cols], V[ks, cols], DAT[qs, cols]
+            dq = dk = dv = None
+            for h in range(2):
+                m = head_mask[h]
+                d_h = d_b * m
+                p = PM[b * 4 + hp * 2 + h]
+                dp = contract(d_h, v_b, 1, 1)
+                ds = (p * (dp - jnp.sum(p * dp, axis=1, keepdims=True))).astype(BF)
+                one = (contract(ds, k_b * m, 1, 0), contract(ds, q_b * m, 0, 0), contract(p.astype(BF), d_h, 0, 0))
+                dq, dk, dv = one if dq is None else (dq + one[0], dk + one[1], dv + one[2])
+            DQKV[qs, cols] = (dq * 0.125).astype(BF)
+            DK[ks, cols] += dk
+            DV[ks, cols] += dv
+        return carry
+
+    lax.fori_loop(0, 2, attend_back, 0)
+    HS[:, 0:256] = DK[0:256, :].astype(BF)
+    HS[:, 256:512] = DV[0:256, :].astype(BF)
+    back = net.make(HS, HR, core_nb)
+    net.start(back, c == 1)
+    tick()
+
+    @pl.when(c == 0)
+    def _():
+        back.wait_recv()
+        DK[512:768, :] += HR[:, 0:256].astype(F32)
+        DV[512:768, :] += HR[:, 256:512].astype(F32)
+
+    DQKV[:, 256:512] = DK[256:768, :].astype(BF)
+    DQKV[:, 512:768] = DV[256:768, :].astype(BF)
+    for n in range(4):
+        cols = slice(n * 256, n * 256 + 256)
+        PART[0, :, cols] = contract(DQKV[...], WQKV[cols, :], 1, 1).astype(BF)
+    last = reduce_start(3, 0)
+    for r in range(4):
+        zbufs[4][0][r % 2, r // 2] = contract(XN[:, r * 256 : r * 256 + 256], DQKV[...], 0, 0).astype(BF)
+    lines.append(along_z(zbufs[4], deliver_qkv))
+    lines.append(along_z(zbufs[3], deliver_wo))
+    tick()
+    last[0]()
+    tick()
+    dx = last[1]()
+    v = X[rows(j, 128), :].astype(F32)
+    scale = lax.rsqrt(jnp.mean(v * v, axis=1, keepdims=True) + EPSILON)
+    w = dx * NG1[...]
+    inner = jnp.mean(w * v, axis=1, keepdims=True)
+    GS[...] = DRES[...] + scale * w - v * (scale * scale * scale * inner)
+    GP[0:1, :] = jnp.sum(dx * v * scale, axis=0, keepdims=True)
+    sent_in = send_blocks(GS, gin)
+
+    me = 4 * x + 2 * y + c
+    got = []
+    for d in range(1, NPLANE):
+        xx, yy, cc = flip(x, d & 1), flip(y, d & 2), flip(c, d & 4)
+        copy = net.make(GP.at[:, lanes(2 * xx + cc)], GR.at[me], dev(z, xx, yy, cc))
+        net.start(copy)
+        got.append(copy)
+    keep = local(GP.at[:, lanes(row)], GR.at[me])
+    keep.start()
+    tick()
+    keep.wait()
+    for copy in got:
+        copy.wait_recv()
+    total = GR[0]
+    for d in range(1, NPLANE):
+        total = total + GR[d]
+    GZS[...] = total
+    got = []
+    for d in range(1, nz):
+        copy = net.make(GZS, GZ.at[z], dev((z + d) % nz, x, y, c))
+        net.start(copy)
+        got.append(copy)
+    keep = local(GZS, GZ.at[z])
+    keep.start()
+    tick(2)
+    keep.wait()
+    for copy in got:
+        copy.wait_recv()
+    total = GZ[0]
+    for d in range(1, nz):
+        total = total + GZ[d]
+    gn1[...] = total[0:1, :]
+    gn2[...] = total[1:2, :]
+    tick(30)
+    sent()
+    sent_in()
+    for copy in flushes:
+        copy.wait()
+    net.finish()
+
+
+def fused(nz, tokens, cotangent, seg_ids, norm_one, wq, wk, wv, wo, norm_two, w_gate, w_up, w_down):
+    ff = w_gate.shape[1]
+    ff_half = -(-ff // 512) * 256
+    ff_cut = ff - ff_half
+    vm = pltpu.VMEM
+    zshapes = [(256 * ff_half // 256, 256), (256, ff_half), (256, ff_half), (256, 256), (256, 768)]
+    zscratch = []
+    for rows, cols in zshapes:
+        zscratch += [
+            vm((2, 2, rows, cols), BF),
+            vm((2, rows, cols), BF),
+            vm((2, nz - 1, 2, rows // nz, cols), BF),
+            vm((rows // nz, cols), BF),
+            vm((nz, 2, rows // nz, cols), BF),
+        ]
+    scratch = [
+        vm((512, D), BF), vm((512, D), BF), vm((D, 768), BF), vm((256, D), BF),
+        vm((D, ff_half), BF), vm((D, ff_half), BF), vm((ff_half, D), BF), vm((1, D), F32), vm((1, D), F32),
+        vm((512, D), BF), vm((512, 256), BF), vm((768, 256), BF), vm((768, 256), BF), vm((2, 256, 512), F32),
+        vm((8, 256, 512), F32), vm((512, 256), BF),
+        vm((3, 512, D), BF), vm((4, 2, 128, D), BF), vm((4, 128, D), BF), vm((4, 128, D), BF),
+        vm((512, D), BF), vm((128, D), F32), vm((128, D), F32), vm((512, ff_half), BF), vm((512, ff_half), BF),
+        vm((512, ff_half), BF), vm((512, D), BF), vm((512, 256), BF),
+        vm((768, 256), F32), vm((768, 256), F32), vm((512, 768), BF), vm((256, 512), BF), vm((256, 512), BF),
+        vm((128, D), BF), vm((128, D), F32), vm((8, D), F32), vm((8, 8, 256), F32), vm((nz, 8, 256), F32), vm((8, 256), F32),
+        *zscratch,
+        vm((3, 256, 512), F32), vm((512, 256), F32), vm((256, ff), F32), vm((256, ff), F32), vm((ff, 256), F32),
+        pltpu.SemaphoreType.DMA((220,)), pltpu.SemaphoreType.DMA((220,)), pltpu.SemaphoreType.DMA((40,)),
+    ]
+    hbm, vmem = pl.BlockSpec(memory_space=pl.ANY), pl.BlockSpec(memory_space=pltpu.VMEM)
+    sds = jax.ShapeDtypeStruct
+    outs = (
+        sds((512, 256), BF), sds((512, 256), F32), sds((1, 256), F32),
+        sds((256, 512), F32), sds((256, 512), F32), sds((256, 512), F32), sds((512, 256), F32),
+        sds((1, 256), F32), sds((256, ff), F32), sds((256, ff), F32), sds((ff, 256), F32),
+    )
+    res = pl.pallas_call(
+        functools.partial(layer_kernel, nz, ff_half, ff_cut),
+        out_shape=outs,
+        in_specs=[hbm, hbm, vmem, vmem, hbm, hbm, hbm, hbm, vmem, hbm, hbm, hbm],
+        out_specs=(hbm, hbm, vmem, hbm, hbm, hbm, hbm, vmem, hbm, hbm, hbm),
+        scratch_shapes=scratch,
+        compiler_params=pltpu.CompilerParams(collective_id=0, has_side_effects=True, vmem_limit_bytes=62 << 20),
+        name="layer",
+    )(
+        tokens, cotangent, seg_ids, norm_one[None], wq, wk, wv, wo, norm_two[None], w_gate, w_up, w_down,
+    )
+    res = list(res)
+    res[2], res[7] = res[2][0], res[7][0]
+    return tuple(res)
+
+
 def solution(mesh):
     in_specs = (
         P(("dp", "col"), "row"),
@@ -313,6 +989,10 @@
         P("row", "col"),
         P("col", "row"),
     )
+    sizes = dict(mesh.shape)
+    body = per_device
+    if sizes["row"] == 4 and sizes["col"] == 2:
+        body = functools.partial(fused, sizes["dp"])
     return jax.shard_map(
-        per_device, mesh=mesh, in_specs=in_specs, out_specs=out_specs, check_vma=False
-    )
+        body, mesh=mesh, in_specs=in_specs, out_specs=out_specs, check_vma=False
+    )

time: 616 us -> 221 us (0.36)
  waiting for transfers between devices: 417 us -> 0 us
  Pallas kernels: 0 us -> 207 us
  blocking collectives: 78.5 us -> 0 us
  matrix products: 48.5 us -> 0 us
  other arithmetic: 34.5 us -> 0 us
  between operations: 14.2 us -> 0.69 us
    pallas_call x0 -> x1, Pallas kernels: none -> 207 us  [fused(): pl.pallas_call(functools.partial(layer_kernel, nz, ff_half, ff_cut), out_...]
    reduce_scatter x8 -> x0, waiting for transfers between devices: 171 us -> none  [the longest x4 144 us: summed_row(): lax.psum_scatter(array_in.astype(jnp.bfloat16), 'row', scatter_dimension=...]
    all_gather x4 -> x0, waiting for transfers between devices: 127 us -> none  [tokens_row(): lax.all_gather(for_sending(array_in), 'row', axis=0, tiled=True)]
    psum x1 -> x0, waiting for transfers between devices: 117 us -> none  [per_device(): lax.psum(grad_wq.astype(jnp.bfloat16), 'dp').astype(jnp.float32)]
    psum x5 -> x0, blocking collectives: 49 us -> none  [the longest x4 27.7 us: feature_total(): return lax.psum(array_in, 'row')]
    dot_general x18 -> x0, matrix products: 48.5 us -> none  [the longest x4 14.4 us: matmul_nt(): lax.dot_general(first_op, second_op, (((1,), (1,)), ((), ())), preferred_...]
    all_gather x4 -> x0, blocking collectives: 29.5 us -> none  [tokens_col(): return lax.all_gather(array_in, 'col', axis=0, tiled=True)]
    convert_element_type x13 -> x0, other arithmetic: 22.4 us -> none  [the longest x1 3.72 us: swiglu_grads(): (dact * up_pre * sigmoid_gate * (1.0 + gate_pre * (1.0 - sigmoid_gate)))....]
  transfers between devices with their start and end apart: 15 -> 0, of which waited for: 13 -> 0; matrix products, arithmetic and copies ran while one was open for 6% -> 0% of each run, Pallas kernels for 0% -> 0%
where the time goes in v1:
time: 221 us
  Pallas kernels  207 us (94%)
  local copies, waits for them, and re-layouts  12.9 us (6%)
    pallas_call x1, Pallas kernels, fused(): pl.pallas_call(functools.partial(layer_kernel, nz, ff_half, ff_cut), out_...  207 us
    unnamed x29, local copies, waits for them, and re-layouts  12.9 us

profile of v1, /device:TPU:0, one launch (start us, length us, event | category | flops | bytes accessed | tf_op | source)
XLA Modules:
  0.0 221.0 jit_solution(17860014849239479956)
XLA Ops:
  0.6 207.4 %layer.1 = (bf16[512,256]{1,0:T(8,128)(2,1)}, f32[512,256]{1,0:T(8,128)}, f32[1,256]{1,0:T(1,128)}, f32[256,512]{1,0:T(8,128)}, f32[256,512]{1,0:T(8,128)}, /*in...) custom-call(bf16[512,256]{1,0:T(8,128)(2,1)} %refs_0_.1, ...), custom_call_target="tpu_custom_call" | custom-call | tf_op jit(solution)/shard_map/layer/pallas_call | solution.py:948
  208.1 0.0 copy-start.8
  208.1 0.0 copy-start.6
  208.1 0.0 copy-start.5
  208.1 1.8 copy.34
  209.9 0.0 copy-start.4
  209.9 1.9 copy.35
  211.8 0.0 copy-done.8
  211.8 0.6 copy.36
  212.4 0.0 copy-done.6
  212.4 0.0 copy-start.3
  212.4 0.8 copy.37
  213.2 0.0 copy-done.5
  213.2 0.0 copy-start.7
  213.2 0.0 copy-start.2
  213.2 0.8 copy.38
  214.0 0.0 copy-done.4
  214.0 0.8 copy.39
  214.7 0.0 copy-done.3
  214.7 0.8 copy.40
  215.5 0.0 copy-done.7
  215.5 0.6 copy.41
  216.1 0.0 copy-done.2
  216.1 0.0 copy-start.1
  216.1 1.1 copy.42
  217.2 0.8 copy-done.1
  218.0 0.0 copy-start
  218.0 1.1 copy.43
  219.1 0.8 copy-done
  219.9 1.1 copy.44
Async XLA Ops:
  208.1 3.7 %copy-start.8 = (f32[1,256]{1,0:T(1,128)S(1)}, f32[1,256]{1,0:T(1,128)}, u32[]{:S(2)}) copy-start(f32[1,256]{1,0:T(1,128)} %get-tuple-element.24) | copy-start | bytes 3076
  208.1 4.3 %copy-start.6 = (f32[256,512]{1,0:T(8,128)S(1)}, f32[256,512]{1,0:T(8,128)}, u32[]{:S(2)}) copy-start(f32[256,512]{1,0:T(8,128)} %get-tuple-element.47) | copy-start | bytes 1572868
  208.1 5.1 %copy-start.5 = (f32[256,512]{1,0:T(8,128)S(1)}, f32[256,512]{1,0:T(8,128)}, u32[]{:S(2)}) copy-start(f32[256,512]{1,0:T(8,128)} %get-tuple-element.48) | copy-start | bytes 1572868
  209.9 4.1 %copy-start.4 = (f32[256,512]{1,0:T(8,128)S(1)}, f32[256,512]{1,0:T(8,128)}, u32[]{:S(2)}) copy-start(f32[256,512]{1,0:T(8,128)} %get-tuple-element.49) | copy-start | bytes 1572868
  212.4 2.4 %copy-start.3 = (f32[512,256]{1,0:T(8,128)S(1)}, f32[512,256]{1,0:T(8,128)}, u32[]{:S(2)}) copy-start(f32[512,256]{1,0:T(8,128)} %get-tuple-element.50) | copy-start | bytes 1572868
  213.2 2.4 %copy-start.7 = (f32[1,256]{1,0:T(1,128)S(1)}, f32[1,256]{1,0:T(1,128)}, u32[]{:S(2)}) copy-start(f32[1,256]{1,0:T(1,128)} %get-tuple-element.29) | copy-start | bytes 3076
  213.2 3.0 %copy-start.2 = (f32[256,1408]{1,0:T(8,128)S(1)}, f32[256,1408]{1,0:T(8,128)}, u32[]{:S(2)}) copy-start(f32[256,1408]{1,0:T(8,128)} %get-tuple-element.52) | copy-start | bytes 4325380
  216.1 1.9 copy-start.1
  218.0 1.9 copy-start

commit v2 on v1

--- a/solution.py
+++ b/solution.py
@@ -339,15 +339,14 @@
     it = iter(refs)
     take = lambda n: [next(it) for _ in range(n)]
     tok, cot, seg, n1, wq, wk, wv, wo, n2, wg, wu, wd = take(12)
-    out, gin, gn1, gwq, gwk, gwv, gwo, gn2, gwg, gwu, gwd = take(11)
+    out, gin, gains, fd, fg, fu, fo, fq = take(8)
     X, G, WQKV, WO, WG, WU, WD, NG1, NG2 = take(9)
-    XN, Q, K, V, BIAS, PM, A = take(7)
-    PART, RY, RX, SX = take(4)
+    XN, Q, K, V, BIAS, PM, AF = take(7)
+    PART, RA, RB, R2, S2 = take(5)
     HN, RES, DRES, ACT, DGA, DUP, DB, DAT = take(8)
     DK, DV, DQKV, HS, HR = take(5)
     OS, GS, GP, GR, GZ, GZS = take(6)
     zbufs = [take(5) for _ in range(5)]
-    OFQ, OFO, OFF1, OFF2, OFD = take(5)
     send, recv, loc = take(3)
 
     z, row, y = lax.axis_index("dp"), lax.axis_index("row"), lax.axis_index("col")
@@ -380,37 +379,51 @@
     def gather_tokens(src, buf):
         col = lambda rr: buf.at[:, lanes(rr)]
         mine = c == y
+        other = jnp.logical_not(mine)
         keep = local(src, col(row))
-        pl.when(mine)(keep.start)
         over = net.make(src, col(row), core_nb)
-        bx, by, bf = net.take(2), net.take(2), net.take(2)
-        net.start(net.make(src, col(row), dev(z, 1 - x, y, y), bx + c))
-        net.start(net.make(src, col(row), dev(z, x, 1 - y, y), by + c))
-        net.start(over, jnp.logical_not(mine))
-        fw = [net.make(col(2 * (1 - x) + k), col(2 * (1 - x) + k), y_nb, bf + k) for k in range(2)]
-        inx = [net.make(src, col(row), core_nb, bx + k) for k in range(2)]
-        iny = [net.make(src, col(row), core_nb, by + k) for k in range(2)]
+        bx, by = net.take(2), net.take(2)
+        to_x = net.make(src, col(row), dev(z, 1 - x, y, y), bx + c)
+        to_y = net.make(src, col(row), dev(z, x, 1 - y, y), by + c)
+        far = 2 * (1 - x)
+        by_y = net.make(col(far), col(far), y_nb)
+        by_x = net.make(col(2 * x + 1), col(2 * x + 1), x_nb)
+        got_x = [net.make(src, col(row), core_nb, bx + k) for k in range(2)]
+        got_y = [net.make(src, col(row), core_nb, by + k) for k in range(2)]
+
+        def start():
+            pl.when(mine)(keep.start)
+            net.start(to_x)
+            net.start(to_y)
+            net.start(over, other)
 
         def arrive():
             @pl.when(mine)
             def _():
-                for k in range(2):
-                    inx[k].wait_recv()
-                    fw[k].start()
+                got_x[0].wait_recv()
+                by_y.start()
+
+            @pl.when(other)
+            def _():
+                got_y[1].wait_recv()
+                by_x.start()
+
+            net.open += [(by_y, mine), (by_x, other)]
+
+        def rest():
+            @pl.when(mine)
+            def _():
+                got_x[1].wait_recv()
                 over.wait_recv()
                 keep.wait()
 
-            net.open += [(f, mine) for f in fw]
-
-        def rest():
-            @pl.when(jnp.logical_not(mine))
+            @pl.when(other)
             def _():
-                for k in range(2):
-                    iny[k].wait_recv()
-                for k in range(2):
-                    fw[k].wait_recv()
-
-        return arrive, rest
+                got_y[0].wait_recv()
+                by_y.wait_recv()
+                by_x.wait_recv()
+
+        return start, arrive, rest
 
     def relay(src_of, dst_of):
         keep = local(src_of(x), dst_of(row))
@@ -434,6 +447,73 @@
             fwd.wait_recv()
 
         return start, arrive, rest
+
+    def relay_z(src_of, dst_of, n_rows):
+        n = n_rows // nz
+        keep = local(src_of(x, 0, n_rows), dst_of(row, 0, n_rows))
+        across = net.make(src_of(x, 0, n_rows), dst_of(row, 0, n_rows), core_nb)
+        far = net.make(src_of(1 - x, z * n, n), dst_of(row, z * n, n), x_nb)
+        theirs = lambda q: dst_of(2 * (1 - x) + c, q * n, n)
+        spread = [net.make(theirs(z), theirs(z), dev((z + d) % nz, x, y, c)) for d in range(1, nz)]
+        whole = dst_of(2 * (1 - x) + c, 0, n_rows)
+        fwd = net.make(whole, whole, core_nb)
+
+        def start():
+            net.start(far)
+            keep.start()
+            net.start(across)
+
+        def arrive():
+            far.wait_recv()
+            for copy in spread:
+                net.start(copy)
+
+        def pass_on():
+            for copy in spread:
+                copy.wait_recv()
+            net.start(fwd)
+
+        def rest():
+            keep.wait()
+            across.wait_recv()
+            fwd.wait_recv()
+
+        return start, arrive, pass_on, rest
+
+    def gather_wo():
+        at = lambda yy, rr: WO.at[rows(yy, 512), lanes(rr)]
+        keep = local(wo, at(y, row))
+        across = net.make(wo, at(y, row), core_nb)
+        to_x, to_y = net.make(wo, at(y, row), x_nb), net.make(wo, at(y, row), y_nb)
+        rx = 2 * (1 - x) + c
+        on_y = net.make(at(y, rx), at(y, rx), y_nb)
+        others = (at(y, rx), at(1 - y, row), at(1 - y, rx))
+        fwd = [net.make(ref, ref, core_nb) for ref in others]
+
+        def start():
+            net.start(to_x)
+            net.start(to_y)
+            keep.start()
+            net.start(across)
+
+        def arrive():
+            to_x.wait_recv()
+            net.start(on_y)
+            net.start(fwd[0])
+
+        def pass_on():
+            to_y.wait_recv()
+            net.start(fwd[1])
+            on_y.wait_recv()
+            net.start(fwd[2])
+
+        def rest():
+            keep.wait()
+            across.wait_recv()
+            for copy in fwd:
+                copy.wait_recv()
+
+        return start, arrive, pass_on, rest
 
     def gather_gain(src, dst):
         keep = local(src, dst.at[:, lanes(row)])
@@ -450,27 +530,43 @@
 
         return rest
 
-    gx = gather_tokens(tok, X)
-    rq = [
-        relay(
-            lambda xx, w=w: w.at[:, lanes(xx)],
-            lambda rr, i=i: WQKV.at[rows(rr, 256), pl.ds(i * 256, 256)],
+    gx, gg = gather_tokens(tok, X), gather_tokens(cot, G)
+    qkv_at = lambda rr, r0, n, i: WQKV.at[pl.ds(pl.multiple_of(rr * 256 + r0, 16), n), pl.ds(i * 256, 256)]
+    rq = relay(lambda xx: wq.at[:, lanes(xx)], lambda rr: WQKV.at[rows(rr, 256), pl.ds(0, 256)])
+    rkv = [
+        relay_z(
+            lambda xx, r0, n, w=w: w.at[pl.ds(pl.multiple_of(r0, 16), n), lanes(xx)],
+            lambda rr, r0, n, i=i: qkv_at(rr, r0, n, i),
+            256,
         )
-        for i, w in enumerate((wq, wk, wv))
+        for i, w in ((1, wk), (2, wv))
     ]
-    for r in rq:
+    ro = gather_wo()
+    cut = lambda xx: pl.multiple_of(xx * ff_cut, 128)
+    rff = [
+        relay_z(
+            lambda xx, r0, n, w=w: w.at[pl.ds(pl.multiple_of(r0, 16), n), pl.ds(cut(xx), ff_half)],
+            lambda rr, r0, n, W=W: W.at[pl.ds(pl.multiple_of(rr * 256 + r0, 16), n), :],
+            256,
+        )
+        for w, W in ((wg, WG), (wu, WU))
+    ]
+    rd = relay_z(
+        lambda xx, r0, n: wd.at[pl.ds(pl.multiple_of(xx * ff_cut + r0, 16), n), :],
+        lambda rr, r0, n: WD.at[pl.ds(pl.multiple_of(r0, 16), n), lanes(rr)],
+        ff_half,
+    )
+    for r in rkv:
         r[0]()
+    gx[0]()
+    rq[0]()
     ga = [gather_gain(n1, NG1), gather_gain(n2, NG2)]
-    gx[0]()
-    gg = gather_tokens(cot, G)
-    ro = relay(lambda xx: wo.at[rows(xx, 256), :], lambda rr: WO.at[:, lanes(rr)])
-    rg = relay(lambda xx: wg.at[:, pl.ds(pl.multiple_of(xx * ff_cut, 128), ff_half)], lambda rr: WG.at[rows(rr, 256), :])
-    ru = relay(lambda xx: wu.at[:, pl.ds(pl.multiple_of(xx * ff_cut, 128), ff_half)], lambda rr: WU.at[rows(rr, 256), :])
-    rd = relay(lambda xx: wd.at[pl.ds(pl.multiple_of(xx * ff_cut, 128), ff_half), :], lambda rr: WD.at[:, lanes(rr)])
-    for r in rq:
+    for r in rkv:
         r[1]()
-    for r in (ro, rg, ru, rd):
+    ro[0]()
+    for r in rff:
         r[0]()
+    gx[1]()
     for _, _, ZR, _, _ in zbufs:
 
         @pl.when(z == 0)
@@ -499,22 +595,30 @@
 
     for g in ga:
         g()
-    gx[1]()
+    gx[2]()
     for t in range(4):
         v = X[t * 128 : t * 128 + 128, :].astype(F32)
         scale = lax.rsqrt(jnp.mean(v * v, axis=1, keepdims=True) + EPSILON)
         XN[t * 128 : t * 128 + 128, :] = (v * scale * NG1[...]).astype(BF)
-    for r in rq:
+    for r in rkv:
         r[2]()
+    for r in rff:
+        r[1]()
+    rd[0]()
+    gg[0]()
+    for r in rkv:
+        r[3]()
     K[256:768, :] = contract(XN[...], WQKV[:, 256:512], 1, 0).astype(BF)
     V[256:768, :] = contract(XN[...], WQKV[:, 512:768], 1, 0).astype(BF)
     hk = net.make(K.at[pl.ds(512, 256), :], K.at[pl.ds(0, 256), :], core_nb)
     hv = net.make(V.at[pl.ds(512, 256), :], V.at[pl.ds(0, 256), :], core_nb)
     net.start(hk, c == 0)
     net.start(hv, c == 0)
+    rq[1]()
+    rq[2]()
     Q[...] = (contract(XN[...], WQKV[:, 0:256], 1, 0).astype(BF) * 0.125).astype(BF)
-
-    gg[0]()
+    ro[1]()
+
     @pl.when(c == 1)
     def _():
         hk.wait_recv()
@@ -523,12 +627,18 @@
     lane_id = lax.broadcasted_iota(jnp.int32, (1, 128), 1)
     head_mask = [jnp.where(lane_id < 64, 1.0, 0.0).astype(BF), jnp.where(lane_id < 64, 0.0, 1.0).astype(BF)]
 
-    def attend(b, carry):
+    heads_at = lambda xx, yy, b: AF.at[pl.ds(b * 256, 256), lanes(2 * yy + xx)]
+    a_x = [net.make(heads_at(x, y, b), heads_at(x, y, b), x_nb) for b in range(2)]
+    a_y = [net.make(heads_at(x, y, b), heads_at(x, y, b), y_nb) for b in range(2)]
+    a_far = (
+        net.make(heads_at(1 - x, y, 0), heads_at(1 - x, y, 0), y_nb),
+        net.make(heads_at(x, 1 - y, 1), heads_at(x, 1 - y, 1), x_nb),
+    )
+    base = (2 * y + x) * 256
+    for b in range(2):
         for hp in range(2):
             cols = slice(hp * 128, hp * 128 + 128)
-            q_b = Q[pl.ds(pl.multiple_of(b * 256, 256), 256), cols]
-            k_b = K[pl.ds(pl.multiple_of(b * 256, 256), 512), cols]
-            v_b = V[pl.ds(pl.multiple_of(b * 256, 256), 512), cols]
+            q_b, k_b, v_b = Q[b * 256 : b * 256 + 256, cols], K[b * 256 : b * 256 + 512, cols], V[b * 256 : b * 256 + 512, cols]
             total = None
             for h in range(2):
                 s = contract(q_b * head_mask[h], k_b, 1, 1) + BIAS[b]
@@ -537,53 +647,73 @@
                 PM[b * 4 + hp * 2 + h] = p
                 part = contract(p.astype(BF), v_b * head_mask[h], 1, 0)
                 total = part if total is None else total + part
-            A[pl.ds(pl.multiple_of(b * 256, 256), 256), cols] = total.astype(BF)
-        return carry
-
-    lax.fori_loop(0, 2, attend, 0)
-    for r in (ro, rg, ru, rd):
-        r[1]()
+            AF[b * 256 : b * 256 + 256, pl.ds(pl.multiple_of(base + hp * 128, 128), 128)] = total.astype(BF)
+        net.start(a_x[b])
+        net.start(a_y[b])
+    for r in rff:
+        r[2]()
+    rd[1]()
+    ro[2]()
+    a_x[0].wait_recv()
+    net.start(a_far[0])
+    a_y[1].wait_recv()
+    net.start(a_far[1])
+    gg[1]()
 
     j = 2 * x + y
     shard = lambda buf, jj: buf.at[rows(jj, 128), :]
 
+    def half(jj, h):
+        return pl.ds(pl.multiple_of(jj * 128 + h * 64, 64), 64)
+
     def reduce_start(k, p):
         part = PART.at[p]
-        a = net.make(shard(part, 2 * (1 - x) + 1 - y), RY.at[k, 0], y_nb)
-        b = net.make(shard(part, 2 * x + 1 - y), RY.at[k, 1], y_nb)
-        d = net.make(SX.at[k], RX.at[k], x_nb)
-        a.start()
-        b.start()
+        j_f, j_x, j_y = 2 * (1 - x) + 1 - y, 2 * (1 - x) + y, 2 * x + 1 - y
+        a = [net.make(part.at[half(q, 0), :], RA.at[k, i], y_nb) for i, q in enumerate((j_f, j_y))]
+        b = [net.make(part.at[half(q, 1), :], RB.at[k, i], x_nb) for i, q in enumerate((j_f, j_x))]
+        sa, sb = net.make(S2.at[k, 0], R2.at[k, 0], x_nb), net.make(S2.at[k, 1], R2.at[k, 1], y_nb)
+        for copy in (a[0], b[0], a[1], b[1]):
+            copy.start()
 
         def mid():
-            a.wait_recv()
-            SX[k] = (PART[p, rows(2 * (1 - x) + y, 128), :].astype(F32) + RY[k, 0].astype(F32)).astype(BF)
-            d.start()
+            a[0].wait_recv()
+            S2[k, 0] = (PART[p, half(j_x, 0), :].astype(F32) + RA[k, 0].astype(F32)).astype(BF)
+            sa.start()
+            b[0].wait_recv()
+            S2[k, 1] = (PART[p, half(j_y, 1), :].astype(F32) + RB[k, 0].astype(F32)).astype(BF)
+            sb.start()
 
         def end():
-            b.wait_recv()
-            d.wait_recv()
-            for copy in (a, b, d):
+            a[1].wait_recv()
+            b[1].wait_recv()
+            sa.wait_recv()
+            sb.wait_recv()
+            for copy in (*a, *b, sa, sb):
                 copy.wait_send()
-            return PART[p, rows(j, 128), :].astype(F32) + RY[k, 1].astype(F32) + RX[k].astype(F32)
+            first = PART[p, half(j, 0), :].astype(F32) + RA[k, 1].astype(F32) + R2[k, 0].astype(F32)
+            second = PART[p, half(j, 1), :].astype(F32) + RB[k, 1].astype(F32) + R2[k, 1].astype(F32)
+            return jnp.concatenate([first, second], axis=0)
 
         return mid, end
 
     def gather_start(buf):
-        a = net.make(shard(buf, j), shard(buf, j), x_nb)
-        b = net.make(shard(buf, j), shard(buf, j), y_nb)
-        jx = 2 * (1 - x) + y
-        f = net.make(shard(buf, jx), shard(buf, jx), y_nb)
-        net.start(a)
-        net.start(b)
+        piece = lambda jj, h: buf.at[half(jj, h), :]
+        to_x = [net.make(piece(j, h), piece(j, h), x_nb) for h in range(2)]
+        to_y = [net.make(piece(j, h), piece(j, h), y_nb) for h in range(2)]
+        j_x, j_y = 2 * (1 - x) + y, 2 * x + 1 - y
+        on_y, on_x = net.make(piece(j_x, 0), piece(j_x, 0), y_nb), net.make(piece(j_y, 1), piece(j_y, 1), x_nb)
+        for copy in (to_x[0], to_y[1], to_x[1], to_y[0]):
+            net.start(copy)
 
         def mid():
-            a.wait_recv()
-            net.start(f)
+            to_x[0].wait_recv()
+            net.start(on_y)
+            to_y[1].wait_recv()
+            net.start(on_x)
 
         def end():
-            b.wait_recv()
-            f.wait_recv()
+            for copy in (to_x[1], to_y[0], on_x, on_y):
+                copy.wait_recv()
 
         return mid, end
 
@@ -629,67 +759,76 @@
 
         return end
 
-    def along_z(bufs, deliver):
+    def along_z(bufs, dst):
         GB, CR, ZR, RL, FF = bufs
         n_rows = CR.shape[1] // nz
-        part = lambda q: CR.at[:, rows(q, n_rows), :]
+        n = n_rows // 2
+        part = lambda q, i: pl.ds(pl.multiple_of(q * n_rows + i * n, 16), n)
+        own = lambda i: pl.ds(i * n, n)
         over = net.make(GB.at[1 - c], CR, core_nb)
-        ends = []
         net.start(over)
         yield
         over.wait_recv()
         for xx in range(2):
             CR[xx] = (CR[xx].astype(F32) + GB[c, xx].astype(F32)).astype(BF)
-        up = [net.take() for _ in range(nz - 1)]
-        dn = [net.take() for _ in range(nz - 1)]
+        sites = [[net.take(nz - 1) for _ in range(2)] for _ in range(2)]
         for s in range(1, nz):
-            for way, sites, to in ((0, up, z_up), (1, dn, z_dn)):
+            for i in range(2):
+                for way, to in ((0, z_up), (1, z_dn)):
+                    zz = z if way == 0 else nz - 1 - z
+                    q = nz - s + zz
+                    q = q if way == 0 else nz - 1 - q
+                    go = (zz < nz - 1) & (zz <= s - 1)
+                    first, later = go & (zz == 0), go & (zz > 0)
+                    site = sites[way][i] + s - 1
+                    there = ZR.at[way, s - 1, :, own(i), :]
+                    net.start(net.make(CR.at[:, part(q, i), :], there, to, site), first)
+                    if s >= 2:
+                        acc = ZR.at[way, s - 2, :, own(i), :]
+                        got = net.make(acc, acc, to, site - 1)
+
+                        @pl.when(later)
+                        def _(got=got, acc=acc, q=q, i=i):
+                            got.wait_recv()
+                            acc[...] = (acc[...].astype(F32) + CR[:, part(q, i), :].astype(F32)).astype(BF)
+
+                        net.start(net.make(acc, there, to, site), later)
+            yield
+        side = []
+        for i in range(2):
+            for way in range(2):
                 zz = z if way == 0 else nz - 1 - z
-                q = nz - s + zz
-                q = q if way == 0 else nz - 1 - q
-                go = (zz < nz - 1) & (zz <= s - 1)
-                first, later = go & (zz == 0), go & (zz > 0)
-                net.start(net.make(part(q), ZR.at[way, s - 1], to, sites[s - 1]), first)
-                if s >= 2:
-                    acc = ZR.at[way, s - 2]
-                    got = net.make(acc, acc, to, sites[s - 2])
-
-                    @pl.when(later)
-                    def _(got=got, acc=acc, q=q):
-                        got.wait_recv()
-                        acc[...] = (acc[...].astype(F32) + CR[:, rows(q, n_rows), :].astype(F32)).astype(BF)
-
-                    net.start(net.make(acc, ZR.at[way, s - 1], to, sites[s - 1]), later)
-            yield
-        for way, sites in ((0, up), (1, dn)):
-            zz = z if way == 0 else nz - 1 - z
-            last = ZR.at[way, nz - 2]
-            pl.when(zz > 0)(net.make(last, last, z_up, sites[nz - 2]).wait_recv)
-        total = lambda xx: (
-            CR[xx, rows(z, n_rows), :].astype(F32) + ZR[0, nz - 2, xx].astype(F32) + ZR[1, nz - 2, xx].astype(F32)
-        ).astype(BF)
-        RL[...] = total(1 - x)
-        side = net.make(RL, FF.at[z, x], x_nb)
-        net.start(side)
-        FF[z, x] = total(x)
+                acc = ZR.at[way, nz - 2, :, own(i), :]
+                pl.when(zz > 0)(net.make(acc, acc, z_up, sites[way][i] + nz - 2).wait_recv)
+            total = lambda xx: (
+                CR[xx, part(z, i), :].astype(F32)
+                + ZR[0, nz - 2, xx, own(i), :].astype(F32)
+                + ZR[1, nz - 2, xx, own(i), :].astype(F32)
+            ).astype(BF)
+            RL[own(i), :] = total(1 - x)
+            side.append(net.make(RL.at[own(i), :], FF.at[z, x, own(i), :], x_nb))
+            net.start(side[i])
+            FF[z, x, own(i), :] = total(x)
         yield
-        side.wait_recv()
-        up = [net.take() for _ in range(nz - 1)]
-        dn = [net.take() for _ in range(nz - 1)]
-        net.start(net.make(FF.at[z], FF.at[z], z_up, up[0]), z < nz - 1)
-        net.start(net.make(FF.at[z], FF.at[z], z_dn, dn[0]), z > 0)
+        sites = [[net.take(nz - 1) for _ in range(2)] for _ in range(2)]
+        here = lambda q, i: FF.at[q, :, own(i), :]
+        for i in range(2):
+            side[i].wait_recv()
+            net.start(net.make(here(z, i), here(z, i), z_up, sites[0][i]), z < nz - 1)
+            net.start(net.make(here(z, i), here(z, i), z_dn, sites[1][i]), z > 0)
         yield
         for s in range(2, nz + 1):
-            for way, sites, to in ((0, up, z_up), (1, dn, z_dn)):
-                zz = z if way == 0 else nz - 1 - z
-                q = z - (s - 1) if way == 0 else z + (s - 1)
-                have = zz >= s - 1
-                got = net.make(FF.at[q], FF.at[q], to, sites[s - 2])
-                pl.when(have)(got.wait_recv)
-                if s < nz:
-                    net.start(net.make(FF.at[q], FF.at[q], to, sites[s - 1]), have & (zz < nz - 1))
+            for i in range(2):
+                for way, to in ((0, z_up), (1, z_dn)):
+                    zz = z if way == 0 else nz - 1 - z
+                    q = z - (s - 1) if way == 0 else z + (s - 1)
+                    have = zz >= s - 1
+                    ref = here(q, i)
+                    pl.when(have)(net.make(ref, ref, to, sites[way][i] + s - 2).wait_recv)
+                    if s < nz:
+                        net.start(net.make(ref, ref, to, sites[way][i] + s - 1), have & (zz < nz - 1))
             yield
-        deliver(FF)
+        flush(FF, dst)
         yield
 
     def flush(buf, dst):
@@ -700,60 +839,35 @@
     flushes = []
     over_cut = ff_half - ff_cut
 
-    def deliver_qkv(FF):
-        for i, dst in enumerate((gwq, gwk, gwv)):
-            for q in range(nz):
-                for xx in range(2):
-                    OFQ[i, q * 64 : q * 64 + 64, xx * 256 : xx * 256 + 256] = FF[q, xx, :, i * 256 : i * 256 + 256].astype(F32)
-            flush(OFQ.at[i], dst)
-
-    def deliver_wo(FF):
-        for q in range(nz):
-            for xx in range(2):
-                OFO[xx * 256 + q * 64 : xx * 256 + q * 64 + 64, :] = FF[q, xx].astype(F32)
-        flush(OFO, gwo)
-
-    def deliver_pair(buf, dst):
-        def run(FF):
-            for q in range(nz):
-                buf[q * 64 : q * 64 + 64, 0:ff_half] = FF[q, 0].astype(F32)
-                buf[q * 64 : q * 64 + 64, ff_half:] = FF[q, 1, :, over_cut:].astype(F32)
-            flush(buf, dst)
-
-        return run
-
-    def deliver_down(FF):
-        n = ff_half // nz
-        for q in range(nz):
-            OFD[q * n : q * n + n, :] = FF[q, 0].astype(F32)
-            skip = max(0, min(n, over_cut - q * n))
-            if skip < n:
-                OFD[ff_cut + q * n + skip : ff_cut + q * n + n, :] = FF[q, 1, skip:, :].astype(F32)
-        flush(OFD, gwd)
-
     lines = []
+
+    def begin(i, dst, wait):
+        line = along_z(zbufs[i], dst)
+        next(line)
+        lines.append([line, wait])
 
     def tick(n=1):
         for _ in range(n):
             for line in lines:
-                next(line, None)
-
-    ro[2]()
-    for n in range(4):
-        PART[0, :, n * 256 : n * 256 + 256] = contract(A[...], WO[:, n * 256 : n * 256 + 256], 1, 0).astype(BF)
-    mid, end = reduce_start(0, 0)
-    mid()
-    gg[1]()
-    res = X[rows(j, 128), :].astype(F32) + end()
-    RES[...] = res
-    scale = lax.rsqrt(jnp.mean(res * res, axis=1, keepdims=True) + EPSILON)
-    HN[rows(j, 128), :] = (res * scale * NG2[...]).astype(BF)
-    mid, end = gather_start(HN)
-    mid()
-    for r in (rg, ru, rd):
-        r[2]()
-    end()
-
+                if line[1] > 0:
+                    line[1] -= 1
+                else:
+                    next(line[0], None)
+
+    ro[3]()
+    for copy in (a_x[1], a_y[0], *a_far):
+        copy.wait_recv()
+    for t in range(4):
+        tile = slice(t * 128, t * 128 + 128)
+        res = X[tile, :].astype(F32) + contract(AF[tile, :], WO[...], 1, 0)
+        RES[tile, :] = res
+        scale = lax.rsqrt(jnp.mean(res * res, axis=1, keepdims=True) + EPSILON)
+        HN[tile, :] = (res * scale * NG2[...]).astype(BF)
+    for r in rff:
+        r[3]()
+    rd[2]()
+    gg[2]()
+    rd[3]()
     skip = (lax.broadcasted_iota(jnp.int32, (1, 256), 1) < over_cut) & (x == 1)
     for n in range(ff_half // 256):
         cols = slice(n * 256, n * 256 + 256)
@@ -768,25 +882,26 @@
         ACT[:, cols] = act.astype(BF)
         DGA[:, cols] = dgate.astype(BF)
         DUP[:, cols] = dup.astype(BF)
+    blocks = lambda i, f: [zbufs[i][0].__setitem__((r % 2, r // 2), f(slice(r * 256, r * 256 + 256)).astype(BF)) for r in range(4)]
+    blocks(0, lambda cols: contract(ACT[...], G[:, cols], 0, 0))
+    begin(0, fd, 0)
+    blocks(1, lambda cols: contract(HN[:, cols], DGA[...], 0, 0))
+    tick()
+    begin(1, fg, 3)
     for n in range(4):
         cols = slice(n * 256, n * 256 + 256)
-        PART[1, :, cols] = (contract(DGA[...], WG[cols, :], 1, 1) + contract(DUP[...], WU[cols, :], 1, 1)).astype(BF)
-    hid = reduce_start(1, 1)
-    for r in range(4):
-        zbufs[0][0][r % 2, r // 2] = contract(ACT[...], G[:, r * 256 : r * 256 + 256], 0, 0).astype(BF)
-    lines.append(along_z(zbufs[0], deliver_down))
+        PART[0, :, cols] = (contract(DGA[...], WG[cols, :], 1, 1) + contract(DUP[...], WU[cols, :], 1, 1)).astype(BF)
+    hid = reduce_start(0, 0)
+    blocks(2, lambda cols: contract(HN[:, cols], DUP[...], 0, 0))
+    begin(2, fu, 7)
     tick()
     for n in range(4):
         cols = slice(n * 256, n * 256 + 256)
-        PART[2, :, cols] = contract(ACT[...], WD[:, cols], 1, 0).astype(BF)
+        PART[1, :, cols] = contract(ACT[...], WD[:, cols], 1, 0).astype(BF)
     hid[0]()
-    fin = reduce_start(2, 2)
-    tick()
-    for r in range(4):
-        zbufs[1][0][r % 2, r // 2] = contract(HN[:, r * 256 : r * 256 + 256], DGA[...], 0, 0).astype(BF)
-    lines.append(along_z(zbufs[1], deliver_pair(OFF1, gwg)))
+    tick()
     dh = hid[1]()
-    res = RES[...]
+    res = RES[rows(j, 128), :]
     scale = lax.rsqrt(jnp.mean(res * res, axis=1, keepdims=True) + EPSILON)
     w = dh * NG2[...]
     inner = jnp.mean(w * res, axis=1, keepdims=True)
@@ -797,19 +912,16 @@
     DB[rows(j, 128), :] = dres.astype(BF)
     dbg = gather_start(DB)
     tick()
-    for r in range(4):
-        zbufs[2][0][r % 2, r // 2] = contract(HN[:, r * 256 : r * 256 + 256], DUP[...], 0, 0).astype(BF)
     dbg[0]()
-    lines.append(along_z(zbufs[2], deliver_pair(OFF2, gwu)))
-    tick()
+    fin = reduce_start(1, 1)
+    tick()
+    dbg[1]()
+
+    DAT[...] = contract(DB[...], WO[pl.ds(pl.multiple_of(base, 256), 256), :], 1, 1).astype(BF)
+    own_heads = AF[:, pl.ds(pl.multiple_of(base, 256), 256)]
+    blocks(3, lambda cols: contract(own_heads, DB[:, cols], 0, 0))
+    begin(3, fo, 8)
     fin[0]()
-    OS[...] = (RES[...] + fin[1]()).astype(BF)
-    sent = send_blocks(OS, out)
-    dbg[1]()
-
-    DAT[...] = contract(DB[...], WO[...], 1, 1).astype(BF)
-    for r in range(4):
-        zbufs[3][0][r % 2, r // 2] = contract(A[...], DB[:, r * 256 : r * 256 + 256], 0, 0).astype(BF)
     tick()
     DK[...] = jnp.zeros_like(DK)
     DV[...] = jnp.zeros_like(DV)
@@ -839,6 +951,8 @@
     back = net.make(HS, HR, core_nb)
     net.start(back, c == 1)
     tick()
+    OS[...] = (RES[rows(j, 128), :] + fin[1]()).astype(BF)
+    sent = send_blocks(OS, out)
 
     @pl.when(c == 0)
     def _():
@@ -848,14 +962,12 @@
 
     DQKV[:, 256:512] = DK[256:768, :].astype(BF)
     DQKV[:, 512:768] = DV[256:768, :].astype(BF)
+    blocks(4, lambda cols: contract(XN[:, cols], DQKV[...], 0, 0))
+    begin(4, fq, 4)
     for n in range(4):
         cols = slice(n * 256, n * 256 + 256)
         PART[0, :, cols] = contract(DQKV[...], WQKV[cols, :], 1, 1).astype(BF)
-    last = reduce_start(3, 0)
-    for r in range(4):
-        zbufs[4][0][r % 2, r // 2] = contract(XN[:, r * 256 : r * 256 + 256], DQKV[...], 0, 0).astype(BF)
-    lines.append(along_z(zbufs[4], deliver_qkv))
-    lines.append(along_z(zbufs[3], deliver_wo))
+    last = reduce_start(2, 0)
     tick()
     last[0]()
     tick()
@@ -899,9 +1011,20 @@
     total = GZ[0]
     for d in range(1, nz):
         total = total + GZ[d]
-    gn1[...] = total[0:1, :]
-    gn2[...] = total[1:2, :]
-    tick(30)
+    gains[...] = total
+    tick()
+    tick()
+    tick()
+    tick()
+    tick()
+    tick()
+    tick()
+    tick()
+    tick()
+    tick()
+    tick()
+    tick()
+    tick(20)
     sent()
     sent_in()
     for copy in flushes:
@@ -909,53 +1032,110 @@
     net.finish()
 
 
+def spread_kernel(nz, ff_half, ff_cut, fd, fg, fu, fo, fq, out_in, gin_in, gains, *refs):
+    out, gin, gn1, gwq, gwk, gwv, gwo, gn2, gwg, gwu, gwd = refs[:11]
+    ID, IG, IU, IO, IQ, OD, OG, OU, OO, OQ, sem, sem_out = refs[11:]
+    over_cut = ff_half - ff_cut
+    passed = [pltpu.make_async_copy(a, b, sem_out.at[i]) for i, (a, b) in enumerate(((out_in, out), (gin_in, gin)))]
+    loads = [pltpu.make_async_copy(a, b, sem.at[i]) for i, (a, b) in enumerate(((fd, ID), (fg, IG), (fu, IU), (fo, IO), (fq, IQ)))]
+    for copy in (*loads, *passed):
+        copy.start()
+    stores = []
+
+    def store(buf, dst):
+        stores.append(pltpu.make_async_copy(buf, dst, sem_out.at[2 + len(stores)]))
+        stores[-1].start()
+
+    gn1[...] = gains[0:1, :]
+    gn2[...] = gains[1:2, :]
+    loads[0].wait()
+    n = ff_half // nz
+    for q in range(nz):
+        OD[q * n : q * n + n, :] = ID[q, 0].astype(F32)
+        skip = max(0, min(n, over_cut - q * n))
+        if skip < n:
+            OD[ff_cut + q * n + skip : ff_cut + q * n + n, :] = ID[q, 1, skip:, :].astype(F32)
+    store(OD, gwd)
+    for k, (I, O, dst) in enumerate(((IG, OG, gwg), (IU, OU, gwu))):
+        loads[1 + k].wait()
+        for q in range(nz):
+            O[q * 64 : q * 64 + 64, 0:ff_half] = I[q, 0].astype(F32)
+            O[q * 64 : q * 64 + 64, ff_half:] = I[q, 1, :, over_cut:].astype(F32)
+        store(O, dst)
+    loads[3].wait()
+    for q in range(nz):
+        for xx in range(2):
+            OO[xx * 256 + q * 64 : xx * 256 + q * 64 + 64, :] = IO[q, xx].astype(F32)
+    store(OO, gwo)
+    loads[4].wait()
+    for i, dst in enumerate((gwq, gwk, gwv)):
+        for q in range(nz):
+            for xx in range(2):
+                OQ[i, q * 64 : q * 64 + 64, xx * 256 : xx * 256 + 256] = IQ[q, xx, :, i * 256 : i * 256 + 256].astype(F32)
+        store(OQ.at[i], dst)
+    for copy in (*passed, *stores):
+        copy.wait()
+
+
 def fused(nz, tokens, cotangent, seg_ids, norm_one, wq, wk, wv, wo, norm_two, w_gate, w_up, w_down):
     ff = w_gate.shape[1]
     ff_half = -(-ff // 512) * 256
     ff_cut = ff - ff_half
     vm = pltpu.VMEM
-    zshapes = [(256 * ff_half // 256, 256), (256, ff_half), (256, ff_half), (256, 256), (256, 768)]
-    zscratch = []
+    zshapes = [(ff_half, 256), (256, ff_half), (256, ff_half), (256, 256), (256, 768)]
+    zscratch, fshapes = [], []
     for rows, cols in zshapes:
+        fshapes.append((nz, 2, rows // nz, cols))
         zscratch += [
             vm((2, 2, rows, cols), BF),
             vm((2, rows, cols), BF),
             vm((2, nz - 1, 2, rows // nz, cols), BF),
             vm((rows // nz, cols), BF),
-            vm((nz, 2, rows // nz, cols), BF),
+            vm(fshapes[-1], BF),
         ]
     scratch = [
-        vm((512, D), BF), vm((512, D), BF), vm((D, 768), BF), vm((256, D), BF),
+        vm((512, D), BF), vm((512, D), BF), vm((D, 768), BF), vm((D, D), BF),
         vm((D, ff_half), BF), vm((D, ff_half), BF), vm((ff_half, D), BF), vm((1, D), F32), vm((1, D), F32),
         vm((512, D), BF), vm((512, 256), BF), vm((768, 256), BF), vm((768, 256), BF), vm((2, 256, 512), F32),
-        vm((8, 256, 512), F32), vm((512, 256), BF),
-        vm((3, 512, D), BF), vm((4, 2, 128, D), BF), vm((4, 128, D), BF), vm((4, 128, D), BF),
-        vm((512, D), BF), vm((128, D), F32), vm((128, D), F32), vm((512, ff_half), BF), vm((512, ff_half), BF),
+        vm((8, 256, 512), F32), vm((512, D), BF),
+        vm((2, 512, D), BF), vm((3, 2, 64, D), BF), vm((3, 2, 64, D), BF), vm((3, 2, 64, D), BF), vm((3, 2, 64, D), BF),
+        vm((512, D), BF), vm((512, D), F32), vm((128, D), F32), vm((512, ff_half), BF), vm((512, ff_half), BF),
         vm((512, ff_half), BF), vm((512, D), BF), vm((512, 256), BF),
         vm((768, 256), F32), vm((768, 256), F32), vm((512, 768), BF), vm((256, 512), BF), vm((256, 512), BF),
         vm((128, D), BF), vm((128, D), F32), vm((8, D), F32), vm((8, 8, 256), F32), vm((nz, 8, 256), F32), vm((8, 256), F32),
         *zscratch,
-        vm((3, 256, 512), F32), vm((512, 256), F32), vm((256, ff), F32), vm((256, ff), F32), vm((ff, 256), F32),
-        pltpu.SemaphoreType.DMA((220,)), pltpu.SemaphoreType.DMA((220,)), pltpu.SemaphoreType.DMA((40,)),
+        pltpu.SemaphoreType.DMA((280,)), pltpu.SemaphoreType.DMA((280,)), pltpu.SemaphoreType.DMA((40,)),
     ]
     hbm, vmem = pl.BlockSpec(memory_space=pl.ANY), pl.BlockSpec(memory_space=pltpu.VMEM)
     sds = jax.ShapeDtypeStruct
-    outs = (
-        sds((512, 256), BF), sds((512, 256), F32), sds((1, 256), F32),
-        sds((256, 512), F32), sds((256, 512), F32), sds((256, 512), F32), sds((512, 256), F32),
-        sds((1, 256), F32), sds((256, ff), F32), sds((256, ff), F32), sds((ff, 256), F32),
-    )
-    res = pl.pallas_call(
+    done = pl.pallas_call(
         functools.partial(layer_kernel, nz, ff_half, ff_cut),
-        out_shape=outs,
+        out_shape=(sds((512, 256), BF), sds((512, 256), F32), sds((8, 256), F32), *(sds(f, BF) for f in fshapes)),
         in_specs=[hbm, hbm, vmem, vmem, hbm, hbm, hbm, hbm, vmem, hbm, hbm, hbm],
-        out_specs=(hbm, hbm, vmem, hbm, hbm, hbm, hbm, vmem, hbm, hbm, hbm),
+        out_specs=(hbm, hbm, vmem, *(hbm for f in fshapes)),
         scratch_shapes=scratch,
         compiler_params=pltpu.CompilerParams(collective_id=0, has_side_effects=True, vmem_limit_bytes=62 << 20),
         name="layer",
     )(
         tokens, cotangent, seg_ids, norm_one[None], wq, wk, wv, wo, norm_two[None], w_gate, w_up, w_down,
     )
+    out, gin, gains, *sums = done
+    grads = (
+        sds((512, 256), BF), sds((512, 256), F32), sds((1, 256), F32),
+        sds((256, 512), F32), sds((256, 512), F32), sds((256, 512), F32), sds((512, 256), F32),
+        sds((1, 256), F32), sds((256, ff), F32), sds((256, ff), F32), sds((ff, 256), F32),
+    )
+    res = pl.pallas_call(
+        functools.partial(spread_kernel, nz, ff_half, ff_cut),
+        out_shape=grads,
+        in_specs=[hbm] * 7 + [vmem],
+        out_specs=tuple(vmem if i in (2, 7) else hbm for i in range(11)),
+        scratch_shapes=[vm(f, BF) for f in fshapes]
+        + [vm((ff, 256), F32), vm((256, ff), F32), vm((256, ff), F32), vm((512, 256), F32), vm((3, 256, 512), F32)]
+        + [pltpu.SemaphoreType.DMA((5,)), pltpu.SemaphoreType.DMA((9,))],
+        compiler_params=pltpu.CompilerParams(vmem_limit_bytes=32 << 20),
+        name="spread",
+    )(*sums, out, gin, gains)
     res = list(res)
     res[2], res[7] = res[2][0], res[7][0]
     return tuple(res)

time: 221 us -> 197 us (0.89)
  Pallas kernels: 207 us -> 188 us
  local copies, waits for them, and re-layouts: 12.9 us -> 8.16 us
    pallas_call x1, Pallas kernels: 207 us -> 184 us  [fused(): pl.pallas_call(functools.partial(layer_kernel, nz, ff_half, ff_cut), out_...]
    unnamed x29 -> x16, local copies, waits for them, and re-layouts: 12.9 us -> 8.16 us
    pallas_call x0 -> x1, Pallas kernels: none -> 3.86 us  [fused(): pl.pallas_call(functools.partial(spread_kernel, nz, ff_half, ff_cut), out...]
where the time goes in v2:
time: 197 us
  Pallas kernels  188 us (95%)
  local copies, waits for them, and re-layouts  8.16 us (4%)
    pallas_call x1, Pallas kernels, fused(): pl.pallas_call(functools.partial(layer_kernel, nz, ff_half, ff_cut), out_...  184 us
    unnamed x16, local copies, waits for them, and re-layouts  8.16 us

profile of v2, /device:TPU:0, one launch (start us, length us, event | category | flops | bytes accessed | tf_op | source)
XLA Modules:
  0.0 197.0 jit_solution(18022352385151897706)
XLA Ops:
  0.6 184.1 %layer.1 = (bf16[512,256]{1,0:T(8,128)(2,1)}, f32[512,256]{1,0:T(8,128)}, f32[8,256]{1,0:T(8,128)}, bf16[4,2,192,256]{3,2,1,0:T(8,128)(2,1)}, bf16[4,2,64,768]{3...) custom-call(bf16[512,256]{1,0:T(8,128)(2,1)} %refs_0_.1, ...), custom_call_target="tpu_custom_call" | custom-call | tf_op jit(solution)/shard_map/layer/pallas_call | solution.py:1111
  184.8 0.0 copy-start
  184.8 1.1 copy-done
  185.9 0.0 copy-start.1
  185.9 1.1 copy-done.1
  187.1 0.0 copy-start.2
  187.1 1.1 copy-done.2
  188.2 0.0 copy-start.3
  188.2 1.1 copy-done.3
  189.3 0.0 copy-start.4
  189.3 1.0 copy-done.4
  190.4 0.0 copy-start.5
  190.4 0.9 copy-done.5
  191.3 0.0 copy-start.6
  191.3 0.9 copy-done.6
  192.3 0.0 copy-start.7
  192.3 0.7 copy-done.7
  193.0 3.9 %spread.1 = (bf16[512,256]{1,0:T(8,128)(2,1)}, f32[512,256]{1,0:T(8,128)}, f32[1,256]{1,0:T(1,128)}, f32[256,512]{1,0:T(8,128)}, f32[256,512]{1,0:T(8,128)}, /*i...) custom-call(bf16[4,2,192,256]{3,2,1,0:T(8,128)(2,1)S(1)} %copy-done,, ...), custom_call_target="tpu_custom_call" | custom-call | tf_op jit(solution)/shard_map/spread/pallas_call | solution.py:1128
Async XLA Ops:
  184.8 1.1 copy-start
  185.9 1.1 copy-start.1
  187.1 1.1 copy-start.2
  188.2 1.1 copy-start.3
  189.3 1.0 copy-start.4
  190.4 0.9 copy-start.5
  191.3 0.9 copy-start.6
  192.3 0.7 copy-start.7

commit v3 on v2

--- a/solution.py
+++ b/solution.py
@@ -293,6 +293,7 @@
 BF = jnp.bfloat16
 F32 = jnp.float32
 NPLANE = 8
+FWAIT, OWAIT, QWAIT = (0, 4, 8), 6, 2
 
 
 def contract(a, b, ca, cb):
@@ -301,19 +302,20 @@
 
 class Copies:
     def __init__(self, send, recv):
-        self.send, self.recv, self.used, self.open = send, recv, 0, []
+        self.send, self.recv, self.used, self.kept, self.open = send, recv, 0, 1, []
 
     def take(self, amount=1):
         base = self.used
         self.used += amount
         return base
 
-    def make(self, src, dst, to, site=None):
+    def make(self, src, dst, to, site=None, own=False):
         site = self.take() if site is None else site
+        self.kept += own
         return pltpu.make_async_remote_copy(
             src_ref=src,
             dst_ref=dst,
-            send_sem=self.send.at[site],
+            send_sem=self.send.at[self.kept - 1 if own else 0],
             recv_sem=self.recv.at[site],
             device_id=to,
             device_id_type=MESH,
@@ -339,11 +341,11 @@
     it = iter(refs)
     take = lambda n: [next(it) for _ in range(n)]
     tok, cot, seg, n1, wq, wk, wv, wo, n2, wg, wu, wd = take(12)
-    out, gin, gains, fd, fg, fu, fo, fq = take(8)
+    out, gin, gains, f0, f1, f2, fo, fq = take(8)
     X, G, WQKV, WO, WG, WU, WD, NG1, NG2 = take(9)
     XN, Q, K, V, BIAS, PM, AF = take(7)
-    PART, RA, RB, R2, S2 = take(5)
-    HN, RES, DRES, ACT, DGA, DUP, DB, DAT = take(8)
+    PART, RX = take(2)
+    HN, RES, DRES, ACT, DGA, DUP, DB, DAT, BYG, BYU = take(10)
     DK, DV, DQKV, HS, HR = take(5)
     OS, GS, GP, GR, GZ, GZS = take(6)
     zbufs = [take(5) for _ in range(5)]
@@ -374,6 +376,32 @@
         )
     for d in range(1, nz):
         pl.semaphore_signal(barrier, inc=1, device_id=dev((z + d) % nz, x, y, c), device_id_type=MESH)
+    for _, _, ZR, _, _ in zbufs:
+
+        @pl.when(z == 0)
+        def _(ZR=ZR):
+            ZR[0, nz - 2] = jnp.zeros(ZR.shape[2:], BF)
+
+        @pl.when(z == nz - 1)
+        def _(ZR=ZR):
+            ZR[1, nz - 2] = jnp.zeros(ZR.shape[2:], BF)
+
+    seg_f = seg[...].astype(F32)
+    own = jnp.where(c == 0, seg_f[:, :512], seg_f[:, 512:])
+    before = jnp.where(c == 0, jnp.full((1, 256), -1.0, F32), seg_f[:, 256:512])
+    ids = jnp.concatenate([before, own], axis=1)
+    for b in range(2):
+        k_id = jnp.broadcast_to(ids[:, b * 256 : b * 256 + 512], (256, 512))
+        q_id = jnp.broadcast_to(ids[:, 256 + b * 256 : 512 + b * 256], (512, 256)).T
+        q_pos = lax.broadcasted_iota(jnp.int32, (256, 512), 0) + 256
+        k_pos = lax.broadcasted_iota(jnp.int32, (256, 512), 1)
+        BIAS[b] = jnp.where((q_id == k_id) & (k_pos <= q_pos), 0.0, NEGATIVE)
+
+    @pl.when(c == 0)
+    def _():
+        K[0:256, :] = jnp.zeros((256, 256), BF)
+        V[0:256, :] = jnp.zeros((256, 256), BF)
+
     pl.semaphore_wait(barrier, NPLANE - 1 + nz - 1)
 
     def gather_tokens(src, buf):
@@ -448,37 +476,48 @@
 
         return start, arrive, rest
 
+    def z_gather(at):
+        sites = (net.take(nz - 1), net.take(nz - 1))
+
+        def step(s):
+            for way, to in ((0, z_up), (1, z_dn)):
+                zz = z if way == 0 else nz - 1 - z
+                ref = at(z - s if way == 0 else z + s)
+                have = zz >= s
+                if s > 0:
+                    pl.when(have)(net.make(ref, ref, to, sites[way] + s - 1).wait_recv)
+                if s < nz - 1:
+                    net.start(net.make(ref, ref, to, sites[way] + s), have & (zz < nz - 1))
+
+        return step
+
     def relay_z(src_of, dst_of, n_rows):
         n = n_rows // nz
         keep = local(src_of(x, 0, n_rows), dst_of(row, 0, n_rows))
         across = net.make(src_of(x, 0, n_rows), dst_of(row, 0, n_rows), core_nb)
         far = net.make(src_of(1 - x, z * n, n), dst_of(row, z * n, n), x_nb)
-        theirs = lambda q: dst_of(2 * (1 - x) + c, q * n, n)
-        spread = [net.make(theirs(z), theirs(z), dev((z + d) % nz, x, y, c)) for d in range(1, nz)]
+        hop = z_gather(lambda q: dst_of(2 * (1 - x) + c, q * n, n))
         whole = dst_of(2 * (1 - x) + c, 0, n_rows)
         fwd = net.make(whole, whole, core_nb)
 
-        def start():
+        def begin():
             net.start(far)
             keep.start()
             net.start(across)
 
-        def arrive():
-            far.wait_recv()
-            for copy in spread:
-                net.start(copy)
-
-        def pass_on():
-            for copy in spread:
-                copy.wait_recv()
-            net.start(fwd)
+        def step(s):
+            if s == 0:
+                far.wait_recv()
+            hop(s)
+            if s == nz - 1:
+                net.start(fwd)
 
         def rest():
             keep.wait()
             across.wait_recv()
             fwd.wait_recv()
 
-        return start, arrive, pass_on, rest
+        return begin, step, rest
 
     def gather_wo():
         at = lambda yy, rr: WO.at[rows(yy, 512), lanes(rr)]
@@ -532,14 +571,13 @@
 
     gx, gg = gather_tokens(tok, X), gather_tokens(cot, G)
     qkv_at = lambda rr, r0, n, i: WQKV.at[pl.ds(pl.multiple_of(rr * 256 + r0, 16), n), pl.ds(i * 256, 256)]
-    rq = relay(lambda xx: wq.at[:, lanes(xx)], lambda rr: WQKV.at[rows(rr, 256), pl.ds(0, 256)])
-    rkv = [
+    rqkv = [
         relay_z(
             lambda xx, r0, n, w=w: w.at[pl.ds(pl.multiple_of(r0, 16), n), lanes(xx)],
             lambda rr, r0, n, i=i: qkv_at(rr, r0, n, i),
             256,
         )
-        for i, w in ((1, wk), (2, wv))
+        for i, w in ((1, wk), (2, wv), (0, wq))
     ]
     ro = gather_wo()
     cut = lambda xx: pl.multiple_of(xx * ff_cut, 128)
@@ -556,69 +594,35 @@
         lambda rr, r0, n: WD.at[pl.ds(pl.multiple_of(r0, 16), n), lanes(rr)],
         ff_half,
     )
-    for r in rkv:
+    for r in rqkv:
         r[0]()
     gx[0]()
-    rq[0]()
     ga = [gather_gain(n1, NG1), gather_gain(n2, NG2)]
-    for r in rkv:
-        r[1]()
-    ro[0]()
-    for r in rff:
-        r[0]()
+    for r in rqkv:
+        r[1](0)
     gx[1]()
-    for _, _, ZR, _, _ in zbufs:
-
-        @pl.when(z == 0)
-        def _(ZR=ZR):
-            ZR[0, nz - 2] = jnp.zeros(ZR.shape[2:], BF)
-
-        @pl.when(z == nz - 1)
-        def _(ZR=ZR):
-            ZR[1, nz - 2] = jnp.zeros(ZR.shape[2:], BF)
-
-    seg_f = seg[...].astype(F32)
-    own = jnp.where(c == 0, seg_f[:, :512], seg_f[:, 512:])
-    before = jnp.where(c == 0, jnp.full((1, 256), -1.0, F32), seg_f[:, 256:512])
-    ids = jnp.concatenate([before, own], axis=1)
-    for b in range(2):
-        k_id = jnp.broadcast_to(ids[:, b * 256 : b * 256 + 512], (256, 512))
-        q_id = jnp.broadcast_to(ids[:, 256 + b * 256 : 512 + b * 256], (512, 256)).T
-        q_pos = lax.broadcasted_iota(jnp.int32, (256, 512), 0) + 256
-        k_pos = lax.broadcasted_iota(jnp.int32, (256, 512), 1)
-        BIAS[b] = jnp.where((q_id == k_id) & (k_pos <= q_pos), 0.0, NEGATIVE)
-
-    @pl.when(c == 0)
-    def _():
-        K[0:256, :] = jnp.zeros((256, 256), BF)
-        V[0:256, :] = jnp.zeros((256, 256), BF)
-
+    for s in range(1, nz):
+        for r in rqkv:
+            r[1](s)
     for g in ga:
         g()
     gx[2]()
+    for r in rff:
+        r[0]()
+    ro[0]()
     for t in range(4):
         v = X[t * 128 : t * 128 + 128, :].astype(F32)
         scale = lax.rsqrt(jnp.mean(v * v, axis=1, keepdims=True) + EPSILON)
         XN[t * 128 : t * 128 + 128, :] = (v * scale * NG1[...]).astype(BF)
-    for r in rkv:
+    for r in rqkv:
         r[2]()
-    for r in rff:
-        r[1]()
-    rd[0]()
-    gg[0]()
-    for r in rkv:
-        r[3]()
     K[256:768, :] = contract(XN[...], WQKV[:, 256:512], 1, 0).astype(BF)
     V[256:768, :] = contract(XN[...], WQKV[:, 512:768], 1, 0).astype(BF)
     hk = net.make(K.at[pl.ds(512, 256), :], K.at[pl.ds(0, 256), :], core_nb)
     hv = net.make(V.at[pl.ds(512, 256), :], V.at[pl.ds(0, 256), :], core_nb)
     net.start(hk, c == 0)
     net.start(hv, c == 0)
-    rq[1]()
-    rq[2]()
     Q[...] = (contract(XN[...], WQKV[:, 0:256], 1, 0).astype(BF) * 0.125).astype(BF)
-    ro[1]()
-
     @pl.when(c == 1)
     def _():
         hk.wait_recv()
@@ -650,72 +654,58 @@
             AF[b * 256 : b * 256 + 256, pl.ds(pl.multiple_of(base + hp * 128, 128), 128)] = total.astype(BF)
         net.start(a_x[b])
         net.start(a_y[b])
+        if b == 0:
+            for r in rff:
+                r[1](0)
+    rd[0]()
     for r in rff:
-        r[2]()
-    rd[1]()
-    ro[2]()
+        r[1](1)
+    ro[1]()
     a_x[0].wait_recv()
     net.start(a_far[0])
     a_y[1].wait_recv()
     net.start(a_far[1])
-    gg[1]()
+    gg[0]()
+    for r in rff:
+        r[1](2)
+    rd[1](0)
+    ro[2]()
+    for r in rff:
+        r[1](3)
+    rd[1](1)
 
     j = 2 * x + y
     shard = lambda buf, jj: buf.at[rows(jj, 128), :]
 
-    def half(jj, h):
-        return pl.ds(pl.multiple_of(jj * 128 + h * 64, 64), 64)
+    peers = ((x_nb, 2 * (1 - x) + y), (y_nb, 2 * x + 1 - y), (dev(z, 1 - x, 1 - y, c), 2 * (1 - x) + 1 - y))
 
     def reduce_start(k, p):
-        part = PART.at[p]
-        j_f, j_x, j_y = 2 * (1 - x) + 1 - y, 2 * (1 - x) + y, 2 * x + 1 - y
-        a = [net.make(part.at[half(q, 0), :], RA.at[k, i], y_nb) for i, q in enumerate((j_f, j_y))]
-        b = [net.make(part.at[half(q, 1), :], RB.at[k, i], x_nb) for i, q in enumerate((j_f, j_x))]
-        sa, sb = net.make(S2.at[k, 0], R2.at[k, 0], x_nb), net.make(S2.at[k, 1], R2.at[k, 1], y_nb)
-        for copy in (a[0], b[0], a[1], b[1]):
+        sent = [net.make(shard(PART.at[p], jj), RX.at[k, i], to, own=True) for i, (to, jj) in enumerate(peers)]
+        for copy in (sent[2], sent[0], sent[1]):
             copy.start()
 
-        def mid():
-            a[0].wait_recv()
-            S2[k, 0] = (PART[p, half(j_x, 0), :].astype(F32) + RA[k, 0].astype(F32)).astype(BF)
-            sa.start()
-            b[0].wait_recv()
-            S2[k, 1] = (PART[p, half(j_y, 1), :].astype(F32) + RB[k, 0].astype(F32)).astype(BF)
-            sb.start()
-
         def end():
-            a[1].wait_recv()
-            b[1].wait_recv()
-            sa.wait_recv()
-            sb.wait_recv()
-            for copy in (*a, *b, sa, sb):
+            for copy in sent:
+                copy.wait_recv()
+            for copy in sent:
                 copy.wait_send()
-            first = PART[p, half(j, 0), :].astype(F32) + RA[k, 1].astype(F32) + R2[k, 0].astype(F32)
-            second = PART[p, half(j, 1), :].astype(F32) + RB[k, 1].astype(F32) + R2[k, 1].astype(F32)
-            return jnp.concatenate([first, second], axis=0)
-
-        return mid, end
+            total = PART[p, rows(j, 128), :].astype(F32)
+            for i in range(3):
+                total = total + RX[k, i].astype(F32)
+            return total
+
+        return end
 
     def gather_start(buf):
-        piece = lambda jj, h: buf.at[half(jj, h), :]
-        to_x = [net.make(piece(j, h), piece(j, h), x_nb) for h in range(2)]
-        to_y = [net.make(piece(j, h), piece(j, h), y_nb) for h in range(2)]
-        j_x, j_y = 2 * (1 - x) + y, 2 * x + 1 - y
-        on_y, on_x = net.make(piece(j_x, 0), piece(j_x, 0), y_nb), net.make(piece(j_y, 1), piece(j_y, 1), x_nb)
-        for copy in (to_x[0], to_y[1], to_x[1], to_y[0]):
+        sent = [net.make(shard(buf, j), shard(buf, j), to) for to, _ in peers]
+        for copy in (sent[2], sent[0], sent[1]):
             net.start(copy)
 
-        def mid():
-            to_x[0].wait_recv()
-            net.start(on_y)
-            to_y[1].wait_recv()
-            net.start(on_x)
-
         def end():
-            for copy in (to_x[1], to_y[0], on_x, on_y):
+            for copy in sent:
                 copy.wait_recv()
 
-        return mid, end
+        return end
 
     def send_blocks(src, dst):
         base_r = net.take(4)
@@ -724,11 +714,10 @@
             for cc in range(2):
                 xx = flip(x, dx)
                 piece, place = src.at[:, lanes(2 * xx + cc)], dst.at[rows(j, 128), :]
-                s = net.take()
                 copy = pltpu.make_async_remote_copy(
                     src_ref=piece,
                     dst_ref=place,
-                    send_sem=net.send.at[s],
+                    send_sem=net.send.at[0],
                     recv_sem=net.recv.at[base_r + dx * 2 + y],
                     device_id=dev(z, xx, c, cc),
                     device_id_type=MESH,
@@ -759,8 +748,8 @@
 
         return end
 
-    def along_z(bufs, dst):
-        GB, CR, ZR, RL, FF = bufs
+    def along_z(tag, dst):
+        GB, CR, ZR, RL, FF = zbufs[tag]
         n_rows = CR.shape[1] // nz
         n = n_rows // 2
         part = lambda q, i: pl.ds(pl.multiple_of(q * n_rows + i * n, 16), n)
@@ -793,7 +782,7 @@
                             acc[...] = (acc[...].astype(F32) + CR[:, part(q, i), :].astype(F32)).astype(BF)
 
                         net.start(net.make(acc, there, to, site), later)
-            yield
+                yield
         side = []
         for i in range(2):
             for way in range(2):
@@ -809,14 +798,14 @@
             side.append(net.make(RL.at[own(i), :], FF.at[z, x, own(i), :], x_nb))
             net.start(side[i])
             FF[z, x, own(i), :] = total(x)
-        yield
+            yield
         sites = [[net.take(nz - 1) for _ in range(2)] for _ in range(2)]
         here = lambda q, i: FF.at[q, :, own(i), :]
         for i in range(2):
             side[i].wait_recv()
             net.start(net.make(here(z, i), here(z, i), z_up, sites[0][i]), z < nz - 1)
             net.start(net.make(here(z, i), here(z, i), z_dn, sites[1][i]), z > 0)
-        yield
+            yield
         for s in range(2, nz + 1):
             for i in range(2):
                 for way, to in ((0, z_up), (1, z_dn)):
@@ -827,7 +816,7 @@
                     pl.when(have)(net.make(ref, ref, to, sites[way][i] + s - 2).wait_recv)
                     if s < nz:
                         net.start(net.make(ref, ref, to, sites[way][i] + s - 1), have & (zz < nz - 1))
-            yield
+                yield
         flush(FF, dst)
         yield
 
@@ -842,17 +831,18 @@
     lines = []
 
     def begin(i, dst, wait):
-        line = along_z(zbufs[i], dst)
+        line = along_z(i, dst)
         next(line)
         lines.append([line, wait])
 
     def tick(n=1):
         for _ in range(n):
-            for line in lines:
-                if line[1] > 0:
-                    line[1] -= 1
-                else:
-                    next(line[0], None)
+            for _ in range(2):
+                for line in lines:
+                    if line[1] > 0:
+                        line[1] -= 1
+                    else:
+                        next(line[0], None)
 
     ro[3]()
     for copy in (a_x[1], a_y[0], *a_far):
@@ -863,44 +853,58 @@
         RES[tile, :] = res
         scale = lax.rsqrt(jnp.mean(res * res, axis=1, keepdims=True) + EPSILON)
         HN[tile, :] = (res * scale * NG2[...]).astype(BF)
+    rd[1](2)
+    gg[1]()
     for r in rff:
-        r[3]()
-    rd[2]()
-    gg[2]()
-    rd[3]()
+        r[2]()
     skip = (lax.broadcasted_iota(jnp.int32, (1, 256), 1) < over_cut) & (x == 1)
+    def tile_grads(n):
+        cols = slice(n * 256, n * 256 + 256)
+        GB = zbufs[n][0]
+        for i, made in enumerate((DGA, DUP)):
+            whole = contract(HN[...], made[:, cols], 0, 0)
+            for r in range(4):
+                GB[r % 2, r // 2, :, i * 256 : i * 256 + 256] = whole[r * 256 : r * 256 + 256].astype(BF)
+        whole = contract(ACT[:, cols], G[...], 0, 0)
+        for r in range(4):
+            GB[r % 2, r // 2, :, 512:768] = whole[:, r * 256 : r * 256 + 256].astype(BF)
+        begin(n, (f0, f1, f2)[n], FWAIT[n])
+
     for n in range(ff_half // 256):
         cols = slice(n * 256, n * 256 + 256)
         gate = contract(HN[...], WG[:, cols], 1, 0)
         up = contract(HN[...], WU[:, cols], 1, 0)
-        dact = contract(G[...], WD[cols, :], 1, 1)
         sig = jax.nn.sigmoid(gate)
         silu = gate * sig
-        act, dgate, dup = silu * up, dact * up * sig * (1.0 + gate * (1.0 - sig)), dact * silu
+        act, by_gate = silu * up, up * sig * (1.0 + gate * (1.0 - sig))
         if n == 0:
-            act, dgate, dup = (jnp.where(skip, 0.0, v) for v in (act, dgate, dup))
+            act, by_gate, silu = (jnp.where(skip, 0.0, v) for v in (act, by_gate, silu))
         ACT[:, cols] = act.astype(BF)
-        DGA[:, cols] = dgate.astype(BF)
-        DUP[:, cols] = dup.astype(BF)
+        BYG[:, cols] = by_gate
+        BYU[:, cols] = silu
+    rd[1](3)
+    gg[2]()
+    rd[2]()
+    for n in range(ff_half // 256):
+        cols = slice(n * 256, n * 256 + 256)
+        dact = contract(G[...], WD[cols, :], 1, 1)
+        DGA[:, cols] = (dact * BYG[:, cols]).astype(BF)
+        DUP[:, cols] = (dact * BYU[:, cols]).astype(BF)
+        tile_grads(n)
+        if n == 1:
+            tick()
     blocks = lambda i, f: [zbufs[i][0].__setitem__((r % 2, r // 2), f(slice(r * 256, r * 256 + 256)).astype(BF)) for r in range(4)]
-    blocks(0, lambda cols: contract(ACT[...], G[:, cols], 0, 0))
-    begin(0, fd, 0)
-    blocks(1, lambda cols: contract(HN[:, cols], DGA[...], 0, 0))
     tick()
-    begin(1, fg, 3)
     for n in range(4):
         cols = slice(n * 256, n * 256 + 256)
         PART[0, :, cols] = (contract(DGA[...], WG[cols, :], 1, 1) + contract(DUP[...], WU[cols, :], 1, 1)).astype(BF)
     hid = reduce_start(0, 0)
-    blocks(2, lambda cols: contract(HN[:, cols], DUP[...], 0, 0))
-    begin(2, fu, 7)
     tick()
     for n in range(4):
         cols = slice(n * 256, n * 256 + 256)
         PART[1, :, cols] = contract(ACT[...], WD[:, cols], 1, 0).astype(BF)
-    hid[0]()
     tick()
-    dh = hid[1]()
+    dh = hid()
     res = RES[rows(j, 128), :]
     scale = lax.rsqrt(jnp.mean(res * res, axis=1, keepdims=True) + EPSILON)
     w = dh * NG2[...]
@@ -912,22 +916,20 @@
     DB[rows(j, 128), :] = dres.astype(BF)
     dbg = gather_start(DB)
     tick()
-    dbg[0]()
+    tick()
+    dbg()
     fin = reduce_start(1, 1)
-    tick()
-    dbg[1]()
 
     DAT[...] = contract(DB[...], WO[pl.ds(pl.multiple_of(base, 256), 256), :], 1, 1).astype(BF)
     own_heads = AF[:, pl.ds(pl.multiple_of(base, 256), 256)]
     blocks(3, lambda cols: contract(own_heads, DB[:, cols], 0, 0))
-    begin(3, fo, 8)
-    fin[0]()
+    begin(3, fo, OWAIT)
     tick()
     DK[...] = jnp.zeros_like(DK)
     DV[...] = jnp.zeros_like(DV)
 
-    def attend_back(b, carry):
-        qs, ks = pl.ds(pl.multiple_of(b * 256, 256), 256), pl.ds(pl.multiple_of(b * 256, 256), 512)
+    def attend_back(b):
+        qs, ks = pl.ds(b * 256, 256), pl.ds(b * 256, 512)
         for hp in range(2):
             cols = slice(hp * 128, hp * 128 + 128)
             q_b, k_b, v_b, d_b = Q[qs, cols], K[ks, cols], V[ks, cols], DAT[qs, cols]
@@ -943,16 +945,14 @@
             DQKV[qs, cols] = (dq * 0.125).astype(BF)
             DK[ks, cols] += dk
             DV[ks, cols] += dv
-        return carry
-
-    lax.fori_loop(0, 2, attend_back, 0)
+
+    attend_back(0)
+    tick()
+    attend_back(1)
     HS[:, 0:256] = DK[0:256, :].astype(BF)
     HS[:, 256:512] = DV[0:256, :].astype(BF)
     back = net.make(HS, HR, core_nb)
     net.start(back, c == 1)
-    tick()
-    OS[...] = (RES[rows(j, 128), :] + fin[1]()).astype(BF)
-    sent = send_blocks(OS, out)
 
     @pl.when(c == 0)
     def _():
@@ -963,15 +963,16 @@
     DQKV[:, 256:512] = DK[256:768, :].astype(BF)
     DQKV[:, 512:768] = DV[256:768, :].astype(BF)
     blocks(4, lambda cols: contract(XN[:, cols], DQKV[...], 0, 0))
-    begin(4, fq, 4)
+    begin(4, fq, QWAIT)
+    tick()
+    OS[...] = (RES[rows(j, 128), :] + fin()).astype(BF)
+    sent = send_blocks(OS, out)
     for n in range(4):
         cols = slice(n * 256, n * 256 + 256)
         PART[0, :, cols] = contract(DQKV[...], WQKV[cols, :], 1, 1).astype(BF)
     last = reduce_start(2, 0)
-    tick()
-    last[0]()
-    tick()
-    dx = last[1]()
+    tick(3)
+    dx = last()
     v = X[rows(j, 128), :].astype(F32)
     scale = lax.rsqrt(jnp.mean(v * v, axis=1, keepdims=True) + EPSILON)
     w = dx * NG1[...]
@@ -989,7 +990,7 @@
         got.append(copy)
     keep = local(GP.at[:, lanes(row)], GR.at[me])
     keep.start()
-    tick()
+    tick(2)
     keep.wait()
     for copy in got:
         copy.wait_recv()
@@ -1004,7 +1005,7 @@
         got.append(copy)
     keep = local(GZS, GZ.at[z])
     keep.start()
-    tick(2)
+    tick(30)
     keep.wait()
     for copy in got:
         copy.wait_recv()
@@ -1012,19 +1013,6 @@
     for d in range(1, nz):
         total = total + GZ[d]
     gains[...] = total
-    tick()
-    tick()
-    tick()
-    tick()
-    tick()
-    tick()
-    tick()
-    tick()
-    tick()
-    tick()
-    tick()
-    tick()
-    tick(20)
     sent()
     sent_in()
     for copy in flushes:
@@ -1032,36 +1020,34 @@
     net.finish()
 
 
-def spread_kernel(nz, ff_half, ff_cut, fd, fg, fu, fo, fq, out_in, gin_in, gains, *refs):
+def spread_kernel(nz, ff_half, ff_cut, f0, f1, f2, fo, fq, out_in, gin_in, gains, *refs):
     out, gin, gn1, gwq, gwk, gwv, gwo, gn2, gwg, gwu, gwd = refs[:11]
-    ID, IG, IU, IO, IQ, OD, OG, OU, OO, OQ, sem, sem_out = refs[11:]
+    I0, I1, I2, IO, IQ, OG, OU, OD, OO, OQ, PO, PG, sem, sem_out = refs[11:]
     over_cut = ff_half - ff_cut
-    passed = [pltpu.make_async_copy(a, b, sem_out.at[i]) for i, (a, b) in enumerate(((out_in, out), (gin_in, gin)))]
-    loads = [pltpu.make_async_copy(a, b, sem.at[i]) for i, (a, b) in enumerate(((fd, ID), (fg, IG), (fu, IU), (fo, IO), (fq, IQ)))]
-    for copy in (*loads, *passed):
+    moves = ((f0, I0), (f1, I1), (f2, I2), (fo, IO), (fq, IQ), (out_in, PO), (gin_in, PG))
+    loads = [pltpu.make_async_copy(a, b, sem.at[i]) for i, (a, b) in enumerate(moves)]
+    for copy in loads:
         copy.start()
     stores = []
 
     def store(buf, dst):
-        stores.append(pltpu.make_async_copy(buf, dst, sem_out.at[2 + len(stores)]))
+        stores.append(pltpu.make_async_copy(buf, dst, sem_out.at[len(stores)]))
         stores[-1].start()
 
     gn1[...] = gains[0:1, :]
     gn2[...] = gains[1:2, :]
-    loads[0].wait()
-    n = ff_half // nz
-    for q in range(nz):
-        OD[q * n : q * n + n, :] = ID[q, 0].astype(F32)
-        skip = max(0, min(n, over_cut - q * n))
-        if skip < n:
-            OD[ff_cut + q * n + skip : ff_cut + q * n + n, :] = ID[q, 1, skip:, :].astype(F32)
-    store(OD, gwd)
-    for k, (I, O, dst) in enumerate(((IG, OG, gwg), (IU, OU, gwu))):
-        loads[1 + k].wait()
+    for n, I in enumerate((I0, I1, I2)):
+        loads[n].wait()
         for q in range(nz):
-            O[q * 64 : q * 64 + 64, 0:ff_half] = I[q, 0].astype(F32)
-            O[q * 64 : q * 64 + 64, ff_half:] = I[q, 1, :, over_cut:].astype(F32)
-        store(O, dst)
+            for xx in range(2):
+                at = xx * ff_cut + n * 256
+                skip = over_cut if xx == 1 and n == 0 else 0
+                OG[q * 64 : q * 64 + 64, at + skip : at + 256] = I[q, xx, :, skip:256].astype(F32)
+                OU[q * 64 : q * 64 + 64, at + skip : at + 256] = I[q, xx, :, 256 + skip : 512].astype(F32)
+                if q * 64 >= skip:
+                    OD[at + q * 64 : at + q * 64 + 64, :] = I[q, xx, :, 512:768].astype(F32)
+    for buf, dst in ((OG, gwg), (OU, gwu), (OD, gwd)):
+        store(buf, dst)
     loads[3].wait()
     for q in range(nz):
         for xx in range(2):
@@ -1073,7 +1059,10 @@
             for xx in range(2):
                 OQ[i, q * 64 : q * 64 + 64, xx * 256 : xx * 256 + 256] = IQ[q, xx, :, i * 256 : i * 256 + 256].astype(F32)
         store(OQ.at[i], dst)
-    for copy in (*passed, *stores):
+    for load, buf, dst in ((loads[5], PO, out), (loads[6], PG, gin)):
+        load.wait()
+        store(buf, dst)
+    for copy in stores:
         copy.wait()
 
 
@@ -1082,7 +1071,7 @@
     ff_half = -(-ff // 512) * 256
     ff_cut = ff - ff_half
     vm = pltpu.VMEM
-    zshapes = [(ff_half, 256), (256, ff_half), (256, ff_half), (256, 256), (256, 768)]
+    zshapes = [(256, 768)] * 3 + [(256, 256), (256, 768)]
     zscratch, fshapes = [], []
     for rows, cols in zshapes:
         fshapes.append((nz, 2, rows // nz, cols))
@@ -1098,13 +1087,13 @@
         vm((D, ff_half), BF), vm((D, ff_half), BF), vm((ff_half, D), BF), vm((1, D), F32), vm((1, D), F32),
         vm((512, D), BF), vm((512, 256), BF), vm((768, 256), BF), vm((768, 256), BF), vm((2, 256, 512), F32),
         vm((8, 256, 512), F32), vm((512, D), BF),
-        vm((2, 512, D), BF), vm((3, 2, 64, D), BF), vm((3, 2, 64, D), BF), vm((3, 2, 64, D), BF), vm((3, 2, 64, D), BF),
+        vm((2, 512, D), BF), vm((3, 3, 128, D), BF),
         vm((512, D), BF), vm((512, D), F32), vm((128, D), F32), vm((512, ff_half), BF), vm((512, ff_half), BF),
-        vm((512, ff_half), BF), vm((512, D), BF), vm((512, 256), BF),
+        vm((512, ff_half), BF), vm((512, D), BF), vm((512, 256), BF), vm((512, ff_half), F32), vm((512, ff_half), F32),
         vm((768, 256), F32), vm((768, 256), F32), vm((512, 768), BF), vm((256, 512), BF), vm((256, 512), BF),
         vm((128, D), BF), vm((128, D), F32), vm((8, D), F32), vm((8, 8, 256), F32), vm((nz, 8, 256), F32), vm((8, 256), F32),
         *zscratch,
-        pltpu.SemaphoreType.DMA((280,)), pltpu.SemaphoreType.DMA((280,)), pltpu.SemaphoreType.DMA((40,)),
+        pltpu.SemaphoreType.DMA((10,)), pltpu.SemaphoreType.DMA((255,)), pltpu.SemaphoreType.DMA((22,)),
     ]
     hbm, vmem = pl.BlockSpec(memory_space=pl.ANY), pl.BlockSpec(memory_space=pltpu.VMEM)
     sds = jax.ShapeDtypeStruct
@@ -1131,9 +1120,9 @@
         in_specs=[hbm] * 7 + [vmem],
         out_specs=tuple(vmem if i in (2, 7) else hbm for i in range(11)),
         scratch_shapes=[vm(f, BF) for f in fshapes]
-        + [vm((ff, 256), F32), vm((256, ff), F32), vm((256, ff), F32), vm((512, 256), F32), vm((3, 256, 512), F32)]
-        + [pltpu.SemaphoreType.DMA((5,)), pltpu.SemaphoreType.DMA((9,))],
-        compiler_params=pltpu.CompilerParams(vmem_limit_bytes=32 << 20),
+        + [vm((256, ff), F32), vm((256, ff), F32), vm((ff, 256), F32), vm((512, 256), F32), vm((3, 256, 512), F32)]
+        + [vm((512, 256), BF), vm((512, 256), F32), pltpu.SemaphoreType.DMA((7,)), pltpu.SemaphoreType.DMA((9,))],
+        compiler_params=pltpu.CompilerParams(vmem_limit_bytes=63 << 20),
         name="spread",
     )(*sums, out, gin, gains)
     res = list(res)

time: 197 us -> 169 us (0.86)
  Pallas kernels: 188 us -> 167 us
  local copies, waits for them, and re-layouts: 8.16 us -> 0 us
    pallas_call x1, Pallas kernels: 184 us -> 162 us  [fused(): pl.pallas_call(functools.partial(layer_kernel, nz, ff_half, ff_cut), out_...]
    unnamed x16 -> x0, local copies, waits for them, and re-layouts: 8.16 us -> none
    pallas_call x1, Pallas kernels: 3.86 us -> 5.98 us  [fused(): pl.pallas_call(functools.partial(spread_kernel, nz, ff_half, ff_cut), out...]
where the time goes in v3:
time: 169 us; the launch traced here: 168 us
  Pallas kernels  167 us (99%)
    pallas_call x1, Pallas kernels, fused(): pl.pallas_call(functools.partial(layer_kernel, nz, ff_half, ff_cut), out_...  162 us
    pallas_call x1, Pallas kernels, fused(): pl.pallas_call(functools.partial(spread_kernel, nz, ff_half, ff_cut), out...  5.98 us

profile of v3, /device:TPU:0, one launch (start us, length us, event | category | flops | bytes accessed | tf_op | source)
XLA Modules:
  0.0 168.3 jit_solution(5910932090213020442)
XLA Ops:
  0.6 161.5 %layer.1 = (bf16[512,256]{1,0:T(8,128)(2,1)}, f32[512,256]{1,0:T(8,128)}, f32[8,256]{1,0:T(8,128)}, bf16[4,2,64,768]{3,2,1,0:T(8,128)(2,1)}, bf16[4,2,64,768]{3,...) custom-call(bf16[512,256]{1,0:T(8,128)(2,1)} %refs_0_.1, ...), custom_call_target="tpu_custom_call" | custom-call | tf_op jit(solution)/shard_map/layer/pallas_call | solution.py:1100
  162.2 6.0 %spread.1 = (bf16[512,256]{1,0:T(8,128)(2,1)}, f32[512,256]{1,0:T(8,128)}, f32[1,256]{1,0:T(1,128)}, f32[256,512]{1,0:T(8,128)}, f32[256,512]{1,0:T(8,128)}, /*i...) custom-call(bf16[4,2,64,768]{3,2,1,0:T(8,128)(2,1)} %get-tuple-eleme, ...), custom_call_target="tpu_custom_call" | custom-call | tf_op jit(solution)/shard_map/spread/pallas_call | solution.py:1117

commit v4 on v3

--- a/solution.py
+++ b/solution.py
@@ -293,7 +293,9 @@
 BF = jnp.bfloat16
 F32 = jnp.float32
 NPLANE = 8
-FWAIT, OWAIT, QWAIT = (0, 4, 8), 6, 2
+LATE = (1, 3, 4)
+NEWFIRST, LAG = True, 4
+FWAIT, OWAIT, QWAIT = (2, 6, 0), 0, 0
 
 
 def contract(a, b, ca, cb):
@@ -345,7 +347,7 @@
     X, G, WQKV, WO, WG, WU, WD, NG1, NG2 = take(9)
     XN, Q, K, V, BIAS, PM, AF = take(7)
     PART, RX = take(2)
-    HN, RES, DRES, ACT, DGA, DUP, DB, DAT, BYG, BYU = take(10)
+    HN, RES, DRES, ACT, DGA, DUP, DB, DAT, BYG, BYU, T3 = take(11)
     DK, DV, DQKV, HS, HR = take(5)
     OS, GS, GP, GR, GZ, GZS = take(6)
     zbufs = [take(5) for _ in range(5)]
@@ -491,30 +493,36 @@
 
         return step
 
-    def relay_z(src_of, dst_of, n_rows):
+    def relay_z(pairs, whole, n_rows):
         n = n_rows // nz
-        keep = local(src_of(x, 0, n_rows), dst_of(row, 0, n_rows))
-        across = net.make(src_of(x, 0, n_rows), dst_of(row, 0, n_rows), core_nb)
-        far = net.make(src_of(1 - x, z * n, n), dst_of(row, z * n, n), x_nb)
-        hop = z_gather(lambda q: dst_of(2 * (1 - x) + c, q * n, n))
-        whole = dst_of(2 * (1 - x) + c, 0, n_rows)
-        fwd = net.make(whole, whole, core_nb)
+        keep = [local(a, b) for a, b in pairs(x, row, 0, n_rows)]
+        across = [net.make(a, b, core_nb) for a, b in pairs(x, row, 0, n_rows)]
+        far = [net.make(a, b, x_nb) for a, b in pairs(1 - x, row, z * n, n)]
+        hop = z_gather(lambda q: whole(2 * (1 - x) + c, q * n, n))
+        theirs = whole(2 * (1 - x) + c, 0, n_rows)
+        fwd = net.make(theirs, theirs, core_nb)
 
         def begin():
-            net.start(far)
-            keep.start()
-            net.start(across)
+            for copy in far:
+                net.start(copy)
+            for copy in keep:
+                copy.start()
+            for copy in across:
+                net.start(copy)
 
         def step(s):
             if s == 0:
-                far.wait_recv()
+                for copy in far:
+                    copy.wait_recv()
             hop(s)
             if s == nz - 1:
                 net.start(fwd)
 
         def rest():
-            keep.wait()
-            across.wait_recv()
+            for copy in keep:
+                copy.wait()
+            for copy in across:
+                copy.wait_recv()
             fwd.wait_recv()
 
         return begin, step, rest
@@ -570,30 +578,34 @@
         return rest
 
     gx, gg = gather_tokens(tok, X), gather_tokens(cot, G)
-    qkv_at = lambda rr, r0, n, i: WQKV.at[pl.ds(pl.multiple_of(rr * 256 + r0, 16), n), pl.ds(i * 256, 256)]
-    rqkv = [
-        relay_z(
-            lambda xx, r0, n, w=w: w.at[pl.ds(pl.multiple_of(r0, 16), n), lanes(xx)],
-            lambda rr, r0, n, i=i: qkv_at(rr, r0, n, i),
-            256,
-        )
-        for i, w in ((1, wk), (2, wv), (0, wq))
-    ]
+    some = lambda r0, n: pl.ds(pl.multiple_of(r0, 16), n)
+    rqkv = []
+    for i, w in ((1, wk), (2, wv), (0, wq)):
+        at = lambda rr, r0, n, i=i: WQKV.at[some(rr * 256 + r0, n), pl.ds(i * 256, 256)]
+        rqkv.append(relay_z(lambda xx, rr, r0, n, w=w, at=at: [(w.at[some(r0, n), lanes(xx)], at(rr, r0, n))], at, 256))
     ro = gather_wo()
-    cut = lambda xx: pl.multiple_of(xx * ff_cut, 128)
-    rff = [
-        relay_z(
-            lambda xx, r0, n, w=w: w.at[pl.ds(pl.multiple_of(r0, 16), n), pl.ds(cut(xx), ff_half)],
-            lambda rr, r0, n, W=W: W.at[pl.ds(pl.multiple_of(rr * 256 + r0, 16), n), :],
-            256,
-        )
-        for w, W in ((wg, WG), (wu, WU))
-    ]
-    rd = relay_z(
-        lambda xx, r0, n: wd.at[pl.ds(pl.multiple_of(xx * ff_cut + r0, 16), n), :],
-        lambda rr, r0, n: WD.at[pl.ds(pl.multiple_of(r0, 16), n), lanes(rr)],
-        ff_half,
-    )
+    both = ff_half - ff_cut
+    rff = []
+    for w, W in ((wg, WG), (wu, WU)):
+        at = lambda rr, r0, n, W=W: W.at[some(rr * 256 + r0, n), :]
+
+        def pairs(xx, rr, r0, n, w=w, W=W):
+            out = []
+            for src, dst, width in ((pl.multiple_of(xx * ff_half, 128), 0, ff_cut), (ff_cut, ff_cut, both)):
+                out.append((w.at[some(r0, n), pl.ds(src, width)], W.at[some(rr * 256 + r0, n), pl.ds(dst, width)]))
+            return out
+
+        rff.append(relay_z(pairs, at, 256))
+
+    def pairs_down(xx, rr, r0, n):
+        if n == ff_half:
+            parts = ((xx * ff_half, 0, ff_cut), (ff_cut, ff_cut, both))
+        else:
+            tail = jnp.where(z == nz - 1, ff_cut, xx * ff_half + r0 + n - both)
+            parts = ((xx * ff_half + r0, r0, n - both), (tail, r0 + n - both, both))
+        return [(wd.at[some(src, k), :], WD.at[some(dst, k), lanes(rr)]) for src, dst, k in parts]
+
+    rd = relay_z(pairs_down, lambda rr, r0, n: WD.at[some(r0, n), lanes(rr)], ff_half)
     for r in rqkv:
         r[0]()
     gx[0]()
@@ -752,14 +764,15 @@
         GB, CR, ZR, RL, FF = zbufs[tag]
         n_rows = CR.shape[1] // nz
         n = n_rows // 2
+        last = CR.shape[0] - 1
         part = lambda q, i: pl.ds(pl.multiple_of(q * n_rows + i * n, 16), n)
         own = lambda i: pl.ds(i * n, n)
         over = net.make(GB.at[1 - c], CR, core_nb)
         net.start(over)
         yield
         over.wait_recv()
-        for xx in range(2):
-            CR[xx] = (CR[xx].astype(F32) + GB[c, xx].astype(F32)).astype(BF)
+        for u in range(CR.shape[0]):
+            CR[u] = (CR[u].astype(F32) + GB[c, u].astype(F32)).astype(BF)
         sites = [[net.take(nz - 1) for _ in range(2)] for _ in range(2)]
         for s in range(1, nz):
             for i in range(2):
@@ -783,29 +796,42 @@
 
                         net.start(net.make(acc, there, to, site), later)
                 yield
+        late = len(RL.shape) == 3
+        backs = [[net.take(nz - 1) for _ in range(2)] for _ in range(2)]
+        here = lambda q, i: FF.at[q, :, own(i), :]
         side = []
+
+        def send_back(i):
+            net.start(net.make(here(z, i), here(z, i), z_up, backs[0][i]), z < nz - 1)
+            net.start(net.make(here(z, i), here(z, i), z_dn, backs[1][i]), z > 0)
+
         for i in range(2):
             for way in range(2):
                 zz = z if way == 0 else nz - 1 - z
                 acc = ZR.at[way, nz - 2, :, own(i), :]
                 pl.when(zz > 0)(net.make(acc, acc, z_up, sites[way][i] + nz - 2).wait_recv)
-            total = lambda xx: (
-                CR[xx, part(z, i), :].astype(F32)
-                + ZR[0, nz - 2, xx, own(i), :].astype(F32)
-                + ZR[1, nz - 2, xx, own(i), :].astype(F32)
+            total = (
+                CR[:, part(z, i), :].astype(F32)
+                + ZR[0, nz - 2, :, own(i), :].astype(F32)
+                + ZR[1, nz - 2, :, own(i), :].astype(F32)
             ).astype(BF)
-            RL[own(i), :] = total(1 - x)
-            side.append(net.make(RL.at[own(i), :], FF.at[z, x, own(i), :], x_nb))
-            net.start(side[i])
-            FF[z, x, own(i), :] = total(x)
+            if late:
+                FF[z, :, own(i), :] = total
+                send_back(i)
+            else:
+                RL[own(i), :] = total[-1]
+                side.append(net.make(RL.at[own(i), :], FF.at[z, last, own(i), :], x_nb))
+                net.start(side[i])
+                FF[z, 0:last, own(i), :] = total[:-1]
             yield
-        sites = [[net.take(nz - 1) for _ in range(2)] for _ in range(2)]
-        here = lambda q, i: FF.at[q, :, own(i), :]
-        for i in range(2):
-            side[i].wait_recv()
-            net.start(net.make(here(z, i), here(z, i), z_up, sites[0][i]), z < nz - 1)
-            net.start(net.make(here(z, i), here(z, i), z_dn, sites[1][i]), z > 0)
-            yield
+        if not late:
+            for i in range(2):
+                side[i].wait_recv()
+                send_back(i)
+                if tag == 4 and i == 1:
+                    gates.append(tag)
+                yield
+        sites = backs
         for s in range(2, nz + 1):
             for i in range(2):
                 for way, to in ((0, z_up), (1, z_dn)):
@@ -817,7 +843,18 @@
                     if s < nz:
                         net.start(net.make(ref, ref, to, sites[way][i] + s - 1), have & (zz < nz - 1))
                 yield
-        flush(FF, dst)
+        if late:
+            trade = net.make(FF.at[:, last], RL, x_nb)
+            while tag in (0, 3) and not gates:
+                yield
+            net.start(trade)
+            for _ in range(LAG):
+                yield
+            trade.wait_recv()
+            flush(FF.at[:, 0:last], dst.at[:, 0:last])
+            flush(RL, dst.at[:, last])
+        else:
+            flush(FF, dst)
         yield
 
     def flush(buf, dst):
@@ -825,8 +862,7 @@
         copy.start()
         flushes.append(copy)
 
-    flushes = []
-    over_cut = ff_half - ff_cut
+    flushes, gates = [], []
 
     lines = []
 
@@ -838,7 +874,7 @@
     def tick(n=1):
         for _ in range(n):
             for _ in range(2):
-                for line in lines:
+                for line in (lines[::-1] if NEWFIRST else lines):
                     if line[1] > 0:
                         line[1] -= 1
                     else:
@@ -857,43 +893,76 @@
     gg[1]()
     for r in rff:
         r[2]()
-    skip = (lax.broadcasted_iota(jnp.int32, (1, 256), 1) < over_cut) & (x == 1)
+    unit = lambda r: jnp.where(x == r // 2, 0, 1)
+    shared = (lax.broadcasted_iota(jnp.int32, (1, 256), 1) >= 256 - both) & (x == 1)
+
     def tile_grads(n):
         cols = slice(n * 256, n * 256 + 256)
         GB = zbufs[n][0]
         for i, made in enumerate((DGA, DUP)):
             whole = contract(HN[...], made[:, cols], 0, 0)
             for r in range(4):
-                GB[r % 2, r // 2, :, i * 256 : i * 256 + 256] = whole[r * 256 : r * 256 + 256].astype(BF)
+                GB[r % 2, unit(r), :, i * 256 : i * 256 + 256] = whole[r * 256 : r * 256 + 256].astype(BF)
         whole = contract(ACT[:, cols], G[...], 0, 0)
         for r in range(4):
-            GB[r % 2, r // 2, :, 512:768] = whole[:, r * 256 : r * 256 + 256].astype(BF)
-        begin(n, (f0, f1, f2)[n], FWAIT[n])
-
-    for n in range(ff_half // 256):
+            GB[r % 2, unit(r), :, 512:768] = whole[:, r * 256 : r * 256 + 256].astype(BF)
+
+    def last_tile_grads(n):
+        GB = zbufs[n][0]
+
+        def put(r, cols, a, b):
+            GB[r % 2, jnp.where(x == r // 2, 0, 2), :, cols] = a.astype(BF)
+
+            @pl.when(x == r // 2)
+            def _():
+                GB[r % 2, 1, :, cols] = b.astype(BF)
+
+        for i in range(2):
+            whole = contract(HN[...], T3[i], 0, 0)
+            for r in range(4):
+                rws = whole[r * 256 : r * 256 + 256]
+                put(r, slice(i * 128, i * 128 + 128), rws[:, :128], rws[:, 128:])
+        whole = contract(T3[2], G[...], 0, 0)
+        for r in range(4):
+            left, right = whole[:, r * 256 : r * 256 + 128], whole[:, r * 256 + 128 : r * 256 + 256]
+            put(
+                r,
+                slice(256, 384),
+                jnp.concatenate([left[:128], right[:128]], axis=0),
+                jnp.concatenate([left[128:], right[128:]], axis=0),
+            )
+
+    tiles = ff_half // 256
+    for n in range(tiles):
         cols = slice(n * 256, n * 256 + 256)
         gate = contract(HN[...], WG[:, cols], 1, 0)
         up = contract(HN[...], WU[:, cols], 1, 0)
         sig = jax.nn.sigmoid(gate)
         silu = gate * sig
-        act, by_gate = silu * up, up * sig * (1.0 + gate * (1.0 - sig))
-        if n == 0:
-            act, by_gate, silu = (jnp.where(skip, 0.0, v) for v in (act, by_gate, silu))
-        ACT[:, cols] = act.astype(BF)
-        BYG[:, cols] = by_gate
+        act = (silu * up).astype(BF)
+        if n == tiles - 1:
+            T3[2] = act
+            act = jnp.where(shared, jnp.zeros_like(act), act)
+        ACT[:, cols] = act
+        BYG[:, cols] = up * sig * (1.0 + gate * (1.0 - sig))
         BYU[:, cols] = silu
     rd[1](3)
     gg[2]()
     rd[2]()
-    for n in range(ff_half // 256):
+    for n in (tiles - 1, *range(tiles - 1)):
         cols = slice(n * 256, n * 256 + 256)
         dact = contract(G[...], WD[cols, :], 1, 1)
-        DGA[:, cols] = (dact * BYG[:, cols]).astype(BF)
-        DUP[:, cols] = (dact * BYU[:, cols]).astype(BF)
-        tile_grads(n)
-        if n == 1:
+        dgate, dup = (dact * BYG[:, cols]).astype(BF), (dact * BYU[:, cols]).astype(BF)
+        if n == tiles - 1:
+            T3[0], T3[1] = dgate, dup
+            dgate, dup = (jnp.where(shared, jnp.zeros_like(v), v) for v in (dgate, dup))
+        DGA[:, cols] = dgate
+        DUP[:, cols] = dup
+        (last_tile_grads if n == tiles - 1 else tile_grads)(n)
+        begin(n, (f0, f1, f2)[n], FWAIT[n])
+        if n == 0:
             tick()
-    blocks = lambda i, f: [zbufs[i][0].__setitem__((r % 2, r // 2), f(slice(r * 256, r * 256 + 256)).astype(BF)) for r in range(4)]
+    blocks = lambda i, f: [zbufs[i][0].__setitem__((r % 2, unit(r)), f(slice(r * 256, r * 256 + 256)).astype(BF)) for r in range(4)]
     tick()
     for n in range(4):
         cols = slice(n * 256, n * 256 + 256)
@@ -924,7 +993,6 @@
     own_heads = AF[:, pl.ds(pl.multiple_of(base, 256), 256)]
     blocks(3, lambda cols: contract(own_heads, DB[:, cols], 0, 0))
     begin(3, fo, OWAIT)
-    tick()
     DK[...] = jnp.zeros_like(DK)
     DV[...] = jnp.zeros_like(DV)
 
@@ -1023,7 +1091,6 @@
 def spread_kernel(nz, ff_half, ff_cut, f0, f1, f2, fo, fq, out_in, gin_in, gains, *refs):
     out, gin, gn1, gwq, gwk, gwv, gwo, gn2, gwg, gwu, gwd = refs[:11]
     I0, I1, I2, IO, IQ, OG, OU, OD, OO, OQ, PO, PG, sem, sem_out = refs[11:]
-    over_cut = ff_half - ff_cut
     moves = ((f0, I0), (f1, I1), (f2, I2), (fo, IO), (fq, IQ), (out_in, PO), (gin_in, PG))
     loads = [pltpu.make_async_copy(a, b, sem.at[i]) for i, (a, b) in enumerate(moves)]
     for copy in loads:
@@ -1036,28 +1103,36 @@
 
     gn1[...] = gains[0:1, :]
     gn2[...] = gains[1:2, :]
-    for n, I in enumerate((I0, I1, I2)):
+    x = lax.axis_index("row") // 2
+    chips = (x, 1 - x)
+    for n, I in enumerate((I0, I1)):
         loads[n].wait()
+        for u, xx in enumerate(chips):
+            at = pl.multiple_of(xx * ff_half + n * 256, 128)
+            for q in range(nz):
+                OG[q * 64 : q * 64 + 64, pl.ds(at, 256)] = I[q, u, :, 0:256].astype(F32)
+                OU[q * 64 : q * 64 + 64, pl.ds(at, 256)] = I[q, u, :, 256:512].astype(F32)
+                OD[pl.ds(at + q * 64, 64), :] = I[q, u, :, 512:768].astype(F32)
+    loads[2].wait()
+    for u, at in enumerate((x * ff_half + ff_half - 256, ff_cut, (1 - x) * ff_half + ff_half - 256)):
+        at = pl.multiple_of(at, 128) if u != 1 else at
         for q in range(nz):
-            for xx in range(2):
-                at = xx * ff_cut + n * 256
-                skip = over_cut if xx == 1 and n == 0 else 0
-                OG[q * 64 : q * 64 + 64, at + skip : at + 256] = I[q, xx, :, skip:256].astype(F32)
-                OU[q * 64 : q * 64 + 64, at + skip : at + 256] = I[q, xx, :, 256 + skip : 512].astype(F32)
-                if q * 64 >= skip:
-                    OD[at + q * 64 : at + q * 64 + 64, :] = I[q, xx, :, 512:768].astype(F32)
+            OG[q * 64 : q * 64 + 64, pl.ds(at, 128)] = I2[q, u, :, 0:128].astype(F32)
+            OU[q * 64 : q * 64 + 64, pl.ds(at, 128)] = I2[q, u, :, 128:256].astype(F32)
+            side = q // 2 * 128
+            OD[pl.ds(at + q % 2 * 64, 64), side : side + 128] = I2[q, u, :, 256:384].astype(F32)
     for buf, dst in ((OG, gwg), (OU, gwu), (OD, gwd)):
         store(buf, dst)
     loads[3].wait()
-    for q in range(nz):
-        for xx in range(2):
-            OO[xx * 256 + q * 64 : xx * 256 + q * 64 + 64, :] = IO[q, xx].astype(F32)
+    for u, xx in enumerate(chips):
+        for q in range(nz):
+            OO[pl.ds(pl.multiple_of(xx * 256, 256) + q * 64, 64), :] = IO[q, u].astype(F32)
     store(OO, gwo)
     loads[4].wait()
     for i, dst in enumerate((gwq, gwk, gwv)):
-        for q in range(nz):
-            for xx in range(2):
-                OQ[i, q * 64 : q * 64 + 64, xx * 256 : xx * 256 + 256] = IQ[q, xx, :, i * 256 : i * 256 + 256].astype(F32)
+        for u, xx in enumerate(chips):
+            for q in range(nz):
+                OQ[i, q * 64 : q * 64 + 64, pl.ds(pl.multiple_of(xx * 256, 256), 256)] = IQ[q, u, :, i * 256 : i * 256 + 256].astype(F32)
         store(OQ.at[i], dst)
     for load, buf, dst in ((loads[5], PO, out), (loads[6], PG, gin)):
         load.wait()
@@ -1071,15 +1146,15 @@
     ff_half = -(-ff // 512) * 256
     ff_cut = ff - ff_half
     vm = pltpu.VMEM
-    zshapes = [(256, 768)] * 3 + [(256, 256), (256, 768)]
+    zshapes = [(2, 256, 768)] * 2 + [(3, 256, 384), (2, 256, 256), (2, 256, 768)]
     zscratch, fshapes = [], []
-    for rows, cols in zshapes:
-        fshapes.append((nz, 2, rows // nz, cols))
+    for units, rows, cols in zshapes:
+        fshapes.append((nz, units, rows // nz, cols))
         zscratch += [
-            vm((2, 2, rows, cols), BF),
-            vm((2, rows, cols), BF),
-            vm((2, nz - 1, 2, rows // nz, cols), BF),
-            vm((rows // nz, cols), BF),
+            vm((2, units, rows, cols), BF),
+            vm((units, rows, cols), BF),
+            vm((2, nz - 1, units, rows // nz, cols), BF),
+            vm((nz, rows // nz, cols) if len(fshapes) in LATE else (rows // nz, cols), BF),
             vm(fshapes[-1], BF),
         ]
     scratch = [
@@ -1089,11 +1164,11 @@
         vm((8, 256, 512), F32), vm((512, D), BF),
         vm((2, 512, D), BF), vm((3, 3, 128, D), BF),
         vm((512, D), BF), vm((512, D), F32), vm((128, D), F32), vm((512, ff_half), BF), vm((512, ff_half), BF),
-        vm((512, ff_half), BF), vm((512, D), BF), vm((512, 256), BF), vm((512, ff_half), F32), vm((512, ff_half), F32),
+        vm((512, ff_half), BF), vm((512, D), BF), vm((512, 256), BF), vm((512, ff_half), F32), vm((512, ff_half), F32), vm((3, 512, 256), BF),
         vm((768, 256), F32), vm((768, 256), F32), vm((512, 768), BF), vm((256, 512), BF), vm((256, 512), BF),
         vm((128, D), BF), vm((128, D), F32), vm((8, D), F32), vm((8, 8, 256), F32), vm((nz, 8, 256), F32), vm((8, 256), F32),
         *zscratch,
-        pltpu.SemaphoreType.DMA((10,)), pltpu.SemaphoreType.DMA((255,)), pltpu.SemaphoreType.DMA((22,)),
+        pltpu.SemaphoreType.DMA((10,)), pltpu.SemaphoreType.DMA((258,)), pltpu.SemaphoreType.DMA((28,)),
     ]
     hbm, vmem = pl.BlockSpec(memory_space=pl.ANY), pl.BlockSpec(memory_space=pltpu.VMEM)
     sds = jax.ShapeDtypeStruct

time: 169 us -> 161 us (0.953)
  Pallas kernels: 167 us -> 159 us
    pallas_call x1, Pallas kernels: 162 us -> 153 us  [fused(): pl.pallas_call(functools.partial(layer_kernel, nz, ff_half, ff_cut), out_...]
where the time goes in v4:
time: 161 us; the launch traced here: 160 us
  Pallas kernels  159 us (99%)
    pallas_call x1, Pallas kernels, fused(): pl.pallas_call(functools.partial(layer_kernel, nz, ff_half, ff_cut), out_...  153 us
    pallas_call x1, Pallas kernels, fused(): pl.pallas_call(functools.partial(spread_kernel, nz, ff_half, ff_cut), out...  5.94 us

profile of v4, /device:TPU:0, one launch (start us, length us, event | category | flops | bytes accessed | tf_op | source)
XLA Modules:
  0.0 160.0 jit_solution(9310293086801260780)
XLA Ops:
  0.6 153.3 %layer.1 = (bf16[512,256]{1,0:T(8,128)(2,1)}, f32[512,256]{1,0:T(8,128)}, f32[8,256]{1,0:T(8,128)}, bf16[4,2,64,768]{3,2,1,0:T(8,128)(2,1)}, bf16[4,2,64,768]{3,...) custom-call(bf16[512,256]{1,0:T(8,128)(2,1)} %refs_0_.1, ...), custom_call_target="tpu_custom_call" | custom-call | tf_op jit(solution)/shard_map/layer/pallas_call | solution.py:1175
  153.9 5.9 %spread.1 = (bf16[512,256]{1,0:T(8,128)(2,1)}, f32[512,256]{1,0:T(8,128)}, f32[1,256]{1,0:T(1,128)}, f32[256,512]{1,0:T(8,128)}, f32[256,512]{1,0:T(8,128)}, /*i...) custom-call(bf16[4,2,64,768]{3,2,1,0:T(8,128)(2,1)} %get-tuple-eleme, ...), custom_call_target="tpu_custom_call" | custom-call | tf_op jit(solution)/shard_map/spread/pallas_call | solution.py:1192

commit v5 on v4

--- a/solution.py
+++ b/solution.py
@@ -293,6 +293,7 @@
 BF = jnp.bfloat16
 F32 = jnp.float32
 NPLANE = 8
+TAIL, HELD = (0, 3), (0, 3)
 LATE = (1, 3, 4)
 NEWFIRST, LAG = True, 4
 FWAIT, OWAIT, QWAIT = (2, 6, 0), 0, 0
@@ -612,15 +613,17 @@
     ga = [gather_gain(n1, NG1), gather_gain(n2, NG2)]
     for r in rqkv:
         r[1](0)
+    for r in rqkv:
+        r[1](1)
     gx[1]()
-    for s in range(1, nz):
+    for s in range(2, nz):
         for r in rqkv:
             r[1](s)
     for g in ga:
         g()
+    for r in (*rff, rd):
+        r[0]()
     gx[2]()
-    for r in rff:
-        r[0]()
     ro[0]()
     for t in range(4):
         v = X[t * 128 : t * 128 + 128, :].astype(F32)
@@ -669,9 +672,9 @@
         if b == 0:
             for r in rff:
                 r[1](0)
-    rd[0]()
     for r in rff:
         r[1](1)
+    rd[1](0)
     ro[1]()
     a_x[0].wait_recv()
     net.start(a_far[0])
@@ -680,11 +683,11 @@
     gg[0]()
     for r in rff:
         r[1](2)
-    rd[1](0)
+    rd[1](1)
     ro[2]()
     for r in rff:
         r[1](3)
-    rd[1](1)
+    rd[1](2)
 
     j = 2 * x + y
     shard = lambda buf, jj: buf.at[rows(jj, 128), :]
@@ -845,7 +848,7 @@
                 yield
         if late:
             trade = net.make(FF.at[:, last], RL, x_nb)
-            while tag in (0, 3) and not gates:
+            while tag in HELD and not gates:
                 yield
             net.start(trade)
             for _ in range(LAG):
@@ -889,10 +892,10 @@
         RES[tile, :] = res
         scale = lax.rsqrt(jnp.mean(res * res, axis=1, keepdims=True) + EPSILON)
         HN[tile, :] = (res * scale * NG2[...]).astype(BF)
-    rd[1](2)
     gg[1]()
     for r in rff:
         r[2]()
+    rd[1](3)
     unit = lambda r: jnp.where(x == r // 2, 0, 1)
     shared = (lax.broadcasted_iota(jnp.int32, (1, 256), 1) >= 256 - both) & (x == 1)
 
@@ -946,7 +949,6 @@
         ACT[:, cols] = act
         BYG[:, cols] = up * sig * (1.0 + gate * (1.0 - sig))
         BYU[:, cols] = silu
-    rd[1](3)
     gg[2]()
     rd[2]()
     for n in (tiles - 1, *range(tiles - 1)):
@@ -1038,14 +1040,15 @@
     for n in range(4):
         cols = slice(n * 256, n * 256 + 256)
         PART[0, :, cols] = contract(DQKV[...], WQKV[cols, :], 1, 1).astype(BF)
+    tick(TAIL[0])
     last = reduce_start(2, 0)
-    tick(3)
+    tick(TAIL[1])
     dx = last()
     v = X[rows(j, 128), :].astype(F32)
     scale = lax.rsqrt(jnp.mean(v * v, axis=1, keepdims=True) + EPSILON)
     w = dx * NG1[...]
     inner = jnp.mean(w * v, axis=1, keepdims=True)
-    GS[...] = DRES[...] + scale * w - v * (scale * scale * scale * inner)
+    GS[...] = (DRES[...] + scale * w - v * (scale * scale * scale * inner)).astype(BF)
     GP[0:1, :] = jnp.sum(dx * v * scale, axis=0, keepdims=True)
     sent_in = send_blocks(GS, gin)
 
@@ -1090,11 +1093,11 @@
 
 def spread_kernel(nz, ff_half, ff_cut, f0, f1, f2, fo, fq, out_in, gin_in, gains, *refs):
     out, gin, gn1, gwq, gwk, gwv, gwo, gn2, gwg, gwu, gwd = refs[:11]
-    I0, I1, I2, IO, IQ, OG, OU, OD, OO, OQ, PO, PG, sem, sem_out = refs[11:]
+    I0, I1, I2, IO, IQ, OG, OU, OD, OO, OQ, PO, PG, PF, sem, sem_out = refs[11:]
     moves = ((f0, I0), (f1, I1), (f2, I2), (fo, IO), (fq, IQ), (out_in, PO), (gin_in, PG))
     loads = [pltpu.make_async_copy(a, b, sem.at[i]) for i, (a, b) in enumerate(moves)]
-    for copy in loads:
-        copy.start()
+    for i in (5, 6, 4, 3, 0, 1, 2):
+        loads[i].start()
     stores = []
 
     def store(buf, dst):
@@ -1105,6 +1108,29 @@
     gn2[...] = gains[1:2, :]
     x = lax.axis_index("row") // 2
     chips = (x, 1 - x)
+    loads[5].wait()
+    store(PO, out)
+    loads[6].wait()
+    PF[...] = PG[...].astype(F32)
+    store(PF, gin)
+    loads[4].wait()
+    for i, dst in enumerate((gwq, gwk, gwv)):
+        for u, xx in enumerate(chips):
+            for q in range(nz):
+                OQ[i, q * 64 : q * 64 + 64, pl.ds(pl.multiple_of(xx * 256, 256), 256)] = IQ[q, u, :, i * 256 : i * 256 + 256].astype(F32)
+        store(OQ.at[i], dst)
+    loads[3].wait()
+    for u, xx in enumerate(chips):
+        for q in range(nz):
+            OO[pl.ds(pl.multiple_of(xx * 256, 256) + q * 64, 64), :] = IO[q, u].astype(F32)
+    store(OO, gwo)
+
+    def store_part(at, width):
+        cols = pl.ds(at, width)
+        store(OG.at[:, cols], gwg.at[:, cols])
+        store(OU.at[:, cols], gwu.at[:, cols])
+        store(OD.at[cols, :], gwd.at[cols, :])
+
     for n, I in enumerate((I0, I1)):
         loads[n].wait()
         for u, xx in enumerate(chips):
@@ -1113,6 +1139,7 @@
                 OG[q * 64 : q * 64 + 64, pl.ds(at, 256)] = I[q, u, :, 0:256].astype(F32)
                 OU[q * 64 : q * 64 + 64, pl.ds(at, 256)] = I[q, u, :, 256:512].astype(F32)
                 OD[pl.ds(at + q * 64, 64), :] = I[q, u, :, 512:768].astype(F32)
+            store_part(at, 256)
     loads[2].wait()
     for u, at in enumerate((x * ff_half + ff_half - 256, ff_cut, (1 - x) * ff_half + ff_half - 256)):
         at = pl.multiple_of(at, 128) if u != 1 else at
@@ -1121,22 +1148,7 @@
             OU[q * 64 : q * 64 + 64, pl.ds(at, 128)] = I2[q, u, :, 128:256].astype(F32)
             side = q // 2 * 128
             OD[pl.ds(at + q % 2 * 64, 64), side : side + 128] = I2[q, u, :, 256:384].astype(F32)
-    for buf, dst in ((OG, gwg), (OU, gwu), (OD, gwd)):
-        store(buf, dst)
-    loads[3].wait()
-    for u, xx in enumerate(chips):
-        for q in range(nz):
-            OO[pl.ds(pl.multiple_of(xx * 256, 256) + q * 64, 64), :] = IO[q, u].astype(F32)
-    store(OO, gwo)
-    loads[4].wait()
-    for i, dst in enumerate((gwq, gwk, gwv)):
-        for u, xx in enumerate(chips):
-            for q in range(nz):
-                OQ[i, q * 64 : q * 64 + 64, pl.ds(pl.multiple_of(xx * 256, 256), 256)] = IQ[q, u, :, i * 256 : i * 256 + 256].astype(F32)
-        store(OQ.at[i], dst)
-    for load, buf, dst in ((loads[5], PO, out), (loads[6], PG, gin)):
-        load.wait()
-        store(buf, dst)
+        store_part(at, 128)
     for copy in stores:
         copy.wait()
 
@@ -1166,7 +1178,7 @@
         vm((512, D), BF), vm((512, D), F32), vm((128, D), F32), vm((512, ff_half), BF), vm((512, ff_half), BF),
         vm((512, ff_half), BF), vm((512, D), BF), vm((512, 256), BF), vm((512, ff_half), F32), vm((512, ff_half), F32), vm((3, 512, 256), BF),
         vm((768, 256), F32), vm((768, 256), F32), vm((512, 768), BF), vm((256, 512), BF), vm((256, 512), BF),
-        vm((128, D), BF), vm((128, D), F32), vm((8, D), F32), vm((8, 8, 256), F32), vm((nz, 8, 256), F32), vm((8, 256), F32),
+        vm((128, D), BF), vm((128, D), BF), vm((8, D), F32), vm((8, 8, 256), F32), vm((nz, 8, 256), F32), vm((8, 256), F32),
         *zscratch,
         pltpu.SemaphoreType.DMA((10,)), pltpu.SemaphoreType.DMA((258,)), pltpu.SemaphoreType.DMA((28,)),
     ]
@@ -1174,7 +1186,7 @@
     sds = jax.ShapeDtypeStruct
     done = pl.pallas_call(
         functools.partial(layer_kernel, nz, ff_half, ff_cut),
-        out_shape=(sds((512, 256), BF), sds((512, 256), F32), sds((8, 256), F32), *(sds(f, BF) for f in fshapes)),
+        out_shape=(sds((512, 256), BF), sds((512, 256), BF), sds((8, 256), F32), *(sds(f, BF) for f in fshapes)),
         in_specs=[hbm, hbm, vmem, vmem, hbm, hbm, hbm, hbm, vmem, hbm, hbm, hbm],
         out_specs=(hbm, hbm, vmem, *(hbm for f in fshapes)),
         scratch_shapes=scratch,
@@ -1196,7 +1208,7 @@
         out_specs=tuple(vmem if i in (2, 7) else hbm for i in range(11)),
         scratch_shapes=[vm(f, BF) for f in fshapes]
         + [vm((256, ff), F32), vm((256, ff), F32), vm((ff, 256), F32), vm((512, 256), F32), vm((3, 256, 512), F32)]
-        + [vm((512, 256), BF), vm((512, 256), F32), pltpu.SemaphoreType.DMA((7,)), pltpu.SemaphoreType.DMA((9,))],
+        + [vm((512, 256), BF), vm((512, 256), BF), vm((512, 256), F32), pltpu.SemaphoreType.DMA((7,)), pltpu.SemaphoreType.DMA((27,))],
         compiler_params=pltpu.CompilerParams(vmem_limit_bytes=63 << 20),
         name="spread",
     )(*sums, out, gin, gains)

time: 161 us -> 158 us (0.981)
  Pallas kernels: 159 us -> 157 us
    pallas_call x1, Pallas kernels: 153 us -> 151 us  [fused(): pl.pallas_call(functools.partial(layer_kernel, nz, ff_half, ff_cut), out_...]
where the time goes in v5:
time: 158 us
  Pallas kernels  157 us (99%)
    pallas_call x1, Pallas kernels, fused(): pl.pallas_call(functools.partial(layer_kernel, nz, ff_half, ff_cut), out_...  151 us
    pallas_call x1, Pallas kernels, fused(): pl.pallas_call(functools.partial(spread_kernel, nz, ff_half, ff_cut), out...  5.54 us

profile of v5, /device:TPU:0, one launch (start us, length us, event | category | flops | bytes accessed | tf_op | source)
XLA Modules:
  0.0 157.6 jit_solution(4272715987178582971)
XLA Ops:
  0.6 151.3 %layer.1 = (bf16[512,256]{1,0:T(8,128)(2,1)}, bf16[512,256]{1,0:T(8,128)(2,1)}, f32[8,256]{1,0:T(8,128)}, bf16[4,2,64,768]{3,2,1,0:T(8,128)(2,1)}, bf16[4,2,64,7...) custom-call(bf16[512,256]{1,0:T(8,128)(2,1)} %refs_0_.1, ...), custom_call_target="tpu_custom_call" | custom-call | tf_op jit(solution)/shard_map/layer/pallas_call | solution.py:1187
  151.9 5.5 %spread.1 = (bf16[512,256]{1,0:T(8,128)(2,1)}, f32[512,256]{1,0:T(8,128)}, f32[1,256]{1,0:T(1,128)}, f32[256,512]{1,0:T(8,128)}, f32[256,512]{1,0:T(8,128)}, /*i...) custom-call(bf16[4,2,64,768]{3,2,1,0:T(8,128)(2,1)} %get-tuple-eleme, ...), custom_call_target="tpu_custom_call" | custom-call | tf_op jit(solution)/shard_map/spread/pallas_call | solution.py:1204

commit v6 on v5

--- a/solution.py
+++ b/solution.py
@@ -293,10 +293,10 @@
 BF = jnp.bfloat16
 F32 = jnp.float32
 NPLANE = 8
-TAIL, HELD = (0, 3), (0, 3)
+TAIL, HELD = (1, 2), (0, 3)
 LATE = (1, 3, 4)
 NEWFIRST, LAG = True, 4
-FWAIT, OWAIT, QWAIT = (2, 6, 0), 0, 0
+FWAIT, OWAIT, QWAIT = (4, 6, 0), 0, 0
 
 
 def contract(a, b, ca, cb):
@@ -1034,12 +1034,12 @@
     DQKV[:, 512:768] = DV[256:768, :].astype(BF)
     blocks(4, lambda cols: contract(XN[:, cols], DQKV[...], 0, 0))
     begin(4, fq, QWAIT)
+    for n in range(4):
+        cols = slice(n * 256, n * 256 + 256)
+        PART[0, :, cols] = contract(DQKV[...], WQKV[cols, :], 1, 1).astype(BF)
     tick()
     OS[...] = (RES[rows(j, 128), :] + fin()).astype(BF)
     sent = send_blocks(OS, out)
-    for n in range(4):
-        cols = slice(n * 256, n * 256 + 256)
-        PART[0, :, cols] = contract(DQKV[...], WQKV[cols, :], 1, 1).astype(BF)
     tick(TAIL[0])
     last = reduce_start(2, 0)
     tick(TAIL[1])

time: 158 us -> 156 us (0.987)
  Pallas kernels: 157 us -> 155 us
    pallas_call x1, Pallas kernels: 151 us -> 149 us  [fused(): pl.pallas_call(functools.partial(layer_kernel, nz, ff_half, ff_cut), out_...]
where the time goes in v6:
time: 156 us
  Pallas kernels  155 us (99%)
    pallas_call x1, Pallas kernels, fused(): pl.pallas_call(functools.partial(layer_kernel, nz, ff_half, ff_cut), out_...  149 us
    pallas_call x1, Pallas kernels, fused(): pl.pallas_call(functools.partial(spread_kernel, nz, ff_half, ff_cut), out...  5.54 us

profile of v6, /device:TPU:0, one launch (start us, length us, event | category | flops | bytes accessed | tf_op | source)
XLA Modules:
  0.0 155.8 jit_solution(7874559536984293516)
XLA Ops:
  0.6 149.4 %layer.1 = (bf16[512,256]{1,0:T(8,128)(2,1)}, bf16[512,256]{1,0:T(8,128)(2,1)}, f32[8,256]{1,0:T(8,128)}, bf16[4,2,64,768]{3,2,1,0:T(8,128)(2,1)}, bf16[4,2,64,7...) custom-call(bf16[512,256]{1,0:T(8,128)(2,1)} %refs_0_.1, ...), custom_call_target="tpu_custom_call" | custom-call | tf_op jit(solution)/shard_map/layer/pallas_call | solution.py:1187
  150.1 5.5 %spread.1 = (bf16[512,256]{1,0:T(8,128)(2,1)}, f32[512,256]{1,0:T(8,128)}, f32[1,256]{1,0:T(1,128)}, f32[256,512]{1,0:T(8,128)}, f32[256,512]{1,0:T(8,128)}, /*i...) custom-call(bf16[4,2,64,768]{3,2,1,0:T(8,128)(2,1)} %get-tuple-eleme, ...), custom_call_target="tpu_custom_call" | custom-call | tf_op jit(solution)/shard_map/spread/pallas_call | solution.py:1204

commit v7 on v6

--- a/solution.py
+++ b/solution.py
@@ -831,7 +831,7 @@
             for i in range(2):
                 side[i].wait_recv()
                 send_back(i)
-                if tag == 4 and i == 1:
+                if tag == 4 and i == 0:
                     gates.append(tag)
                 yield
         sites = backs
@@ -875,8 +875,8 @@
         lines.append([line, wait])
 
     def tick(n=1):
-        for _ in range(n):
-            for _ in range(2):
+        for _ in range(max(1, int(n))):
+            for _ in range(2 if n >= 1 else 1):
                 for line in (lines[::-1] if NEWFIRST else lines):
                     if line[1] > 0:
                         line[1] -= 1
@@ -975,6 +975,7 @@
         cols = slice(n * 256, n * 256 + 256)
         PART[1, :, cols] = contract(ACT[...], WD[:, cols], 1, 0).astype(BF)
     tick()
+    tick(0.5)
     dh = hid()
     res = RES[rows(j, 128), :]
     scale = lax.rsqrt(jnp.mean(res * res, axis=1, keepdims=True) + EPSILON)
@@ -986,7 +987,7 @@
     GP[1:2, :] = jnp.sum(dh * res * scale, axis=0, keepdims=True)
     DB[rows(j, 128), :] = dres.astype(BF)
     dbg = gather_start(DB)
-    tick()
+    tick(0.5)
     tick()
     dbg()
     fin = reduce_start(1, 1)

time: 156 us -> 156 us (level)
  no operation moved by 1% of the time
where the time goes in v7:
time: 156 us
  Pallas kernels  155 us (99%)
    pallas_call x1, Pallas kernels, fused(): pl.pallas_call(functools.partial(layer_kernel, nz, ff_half, ff_cut), out_...  149 us
    pallas_call x1, Pallas kernels, fused(): pl.pallas_call(functools.partial(spread_kernel, nz, ff_half, ff_cut), out...  5.54 us

profile of v7, /device:TPU:0, one launch (start us, length us, event | category | flops | bytes accessed | tf_op | source)
XLA Modules:
  0.0 155.8 jit_solution(1879678891409903398)
XLA Ops:
  0.6 149.4 %layer.1 = (bf16[512,256]{1,0:T(8,128)(2,1)}, bf16[512,256]{1,0:T(8,128)(2,1)}, f32[8,256]{1,0:T(8,128)}, bf16[4,2,64,768]{3,2,1,0:T(8,128)(2,1)}, bf16[4,2,64,7...) custom-call(bf16[512,256]{1,0:T(8,128)(2,1)} %refs_0_.1, ...), custom_call_target="tpu_custom_call" | custom-call | tf_op jit(solution)/shard_map/layer/pallas_call | solution.py:1188
  150.1 5.5 %spread.1 = (bf16[512,256]{1,0:T(8,128)(2,1)}, f32[512,256]{1,0:T(8,128)}, f32[1,256]{1,0:T(1,128)}, f32[256,512]{1,0:T(8,128)}, f32[256,512]{1,0:T(8,128)}, /*i...) custom-call(bf16[4,2,64,768]{3,2,1,0:T(8,128)(2,1)} %get-tuple-eleme, ...), custom_call_target="tpu_custom_call" | custom-call | tf_op jit(solution)/shard_map/spread/pallas_call | solution.py:1205

commit v8 on v6

--- a/solution.py
+++ b/solution.py
@@ -295,7 +295,7 @@
 NPLANE = 8
 TAIL, HELD = (1, 2), (0, 3)
 LATE = (1, 3, 4)
-NEWFIRST, LAG = True, 4
+NEWFIRST, LAG = True, 10
 FWAIT, OWAIT, QWAIT = (4, 6, 0), 0, 0
 
 

time: 156 us -> 156 us (level)
  no operation moved by 1% of the time
where the time goes in v8:
time: 156 us
  Pallas kernels  155 us (99%)
    pallas_call x1, Pallas kernels, fused(): pl.pallas_call(functools.partial(layer_kernel, nz, ff_half, ff_cut), out_...  150 us
    pallas_call x1, Pallas kernels, fused(): pl.pallas_call(functools.partial(spread_kernel, nz, ff_half, ff_cut), out...  5.54 us

profile of v8, /device:TPU:0, one launch (start us, length us, event | category | flops | bytes accessed | tf_op | source)
XLA Modules:
  0.0 156.0 jit_solution(17769723106764204519)
XLA Ops:
  0.6 149.7 %layer.1 = (bf16[512,256]{1,0:T(8,128)(2,1)}, bf16[512,256]{1,0:T(8,128)(2,1)}, f32[8,256]{1,0:T(8,128)}, bf16[4,2,64,768]{3,2,1,0:T(8,128)(2,1)}, bf16[4,2,64,7...) custom-call(bf16[512,256]{1,0:T(8,128)(2,1)} %refs_0_.1, ...), custom_call_target="tpu_custom_call" | custom-call | tf_op jit(solution)/shard_map/layer/pallas_call | solution.py:1187
  150.3 5.5 %spread.1 = (bf16[512,256]{1,0:T(8,128)(2,1)}, f32[512,256]{1,0:T(8,128)}, f32[1,256]{1,0:T(1,128)}, f32[256,512]{1,0:T(8,128)}, f32[256,512]{1,0:T(8,128)}, /*i...) custom-call(bf16[4,2,64,768]{3,2,1,0:T(8,128)(2,1)} %get-tuple-eleme, ...), custom_call_target="tpu_custom_call" | custom-call | tf_op jit(solution)/shard_map/spread/pallas_call | solution.py:1204
